TPU v7x, 32 devices: a whole 2x2x4 slice. The times are simulated.
32 devices in a mesh: batch: 8 (over z, x), head: 4 (over y, core).
Axes of the slice: x: 2, y: 2, z: 4, core: 2. Of those that a mesh axis runs over, the one named last changes fastest.
Arguments:
- tokens: bfloat16 [8, 2048, 768], P('batch', 'head'), may hold values from -6 to 6
- lengths: int32 [8], P('batch'), may hold values from 1024 to 2048, as said below
- w_query: bfloat16 [768, 768], P(None, 'head'), may hold values from -0.3125 to 0.3125
- w_key: bfloat16 [768, 768], P(None, 'head'), may hold values from -0.3125 to 0.3125
- w_value: bfloat16 [768, 768], P(None, 'head'), may hold values from -0.21875 to 0.21875
- w_out: bfloat16 [768, 768], P('head'), may hold values from -0.4375 to 0.4375
- conv_taps: float32 [12, 65], P('head'), may hold values from -0.875 to 0.875
- w_up: bfloat16 [768, 3072], P(None, 'head'), may hold values from -0.21875 to 0.21875
- b_up: float32 [3072], P('head'), may hold values from -3 to 3
- w_down: bfloat16 [3072, 768], P('head'), may hold values from -0.109375 to 0.109375
- gain_attn: float32 [768], replicated, may hold values from 0.5 to 1.5
- shift_attn: float32 [768], replicated, may hold values from -1.75 to 1.75
- gain_ffn: float32 [768], replicated, may hold values from 0.5 to 1.5
- shift_ffn: float32 [768], replicated, may hold values from -1.75 to 1.75
- grad_out: bfloat16 [8, 2048, 768], P('batch', 'head'), may hold values from -6 to 6
Outputs:
- output: bfloat16 [8, 2048, 768], P('batch', 'head')
- d_tokens: float32 [8, 2048, 768], P('batch', 'head')
- d_w_query: float32 [768, 768], P(None, 'head')
- d_w_key: float32 [768, 768], P(None, 'head')
- d_w_value: float32 [768, 768], P(None, 'head')
- d_w_out: float32 [768, 768], P('head')
- d_conv_taps: float32 [12, 65], P('head')
- d_w_up: float32 [768, 3072], P(None, 'head')
- d_b_up: float32 [3072], P('head')
- d_w_down: float32 [3072, 768], P('head')
- d_gain_attn: float32 [768], replicated
- d_shift_attn: float32 [768], replicated
- d_gain_ffn: float32 [768], replicated
- d_shift_ffn: float32 [768], replicated
Inputs may be any that keep to these rules, and one draw needn't show every extreme that they name: `lengths`: the true length of each sequence; in every draw one sequence is exactly 2048 long.
All inputs are finite; a program needn't handle non-finite values.
Results may differ from a plain program's by a relative error of at most 0.015.
Values may be sent and summed in bfloat16 or wider, within the bound.
No kernel may reach another device: no remote copies, remote signals or barrier semaphores. Data moves between devices by JAX's collectives and lax.ppermute only.
A program may use at most 320 MiB of HBM per device.

v0:
```python
import jax
import jax.numpy as jnp
from jax import lax
from jax.sharding import PartitionSpec as P

HEAD_DIM = 64
LANDMARKS = 64
NEWTON = 6


def matmul(left, right):
    return jnp.dot(left, right, precision=lax.Precision.HIGHEST)


def sequence_masks(length, seq_total):
    positions = jnp.arange(seq_total, dtype=jnp.int32)
    landmark_ids = jnp.arange(LANDMARKS + 1, dtype=jnp.int32)
    bounds = landmark_ids * length // LANDMARKS
    member = (positions[None, :] >= bounds[:-1, None]) & (positions[None, :] < bounds[1:, None])
    widths = (bounds[1:] - bounds[:-1]).astype(jnp.float32)
    pool_matrix = member.astype(jnp.float32) / widths[:, None]
    valid_mask = (positions < length).astype(jnp.float32)
    return (valid_mask, pool_matrix)


def newton_inverse(matrix):
    identity = jnp.eye(matrix.shape[0], dtype=matrix.dtype)
    column_top = jnp.max(jnp.sum(matrix, axis=0))
    row_top = jnp.max(jnp.sum(matrix, axis=1))
    iterate = matrix.T / (column_top * row_top)
    for iteration in range(NEWTON):
        product = matmul(matrix, iterate)
        inner = 7.0 * identity - product
        inner = 15.0 * identity - matmul(product, inner)
        inner = 13.0 * identity - matmul(product, inner)
        iterate = 0.25 * matmul(iterate, inner)
    return iterate


def depthwise(values, taps):
    tap_count = taps.shape[0]
    half_width = tap_count // 2
    row_total = values.shape[0]
    padded = jnp.pad(values, ((half_width, half_width), (0, 0)))
    summed = taps[0] * padded[0:row_total]
    for offset in range(1, tap_count):
        summed = summed + taps[offset] * padded[offset : offset + row_total]
    return summed


def nystrom_head(query, key_rows, value_rows, taps, valid_mask, pool_matrix):
    scaling = query.shape[-1] ** (-0.25)
    query_scaled = query * (scaling * valid_mask[:, None])
    key_scaled = key_rows * (scaling * valid_mask[:, None])
    value_masked = value_rows * valid_mask[:, None]
    query_land = matmul(pool_matrix, query_scaled)
    key_land = matmul(pool_matrix, key_scaled)
    first_kernel = jax.nn.softmax(matmul(query_scaled, key_land.T), axis=-1)
    middle_kernel = jax.nn.softmax(matmul(query_land, key_land.T), axis=-1)
    third_scores = matmul(query_land, key_scaled.T)
    third_kernel = jax.nn.softmax(
        jnp.where(valid_mask[None, :] > 0.5, third_scores, -1e30), axis=-1
    )
    inverse = newton_inverse(middle_kernel)
    mixed = matmul(first_kernel, matmul(inverse, matmul(third_kernel, value_masked)))
    return mixed + depthwise(value_masked, taps)


def layer_norm(values, gain, shift):
    centered = values - jnp.mean(values, axis=-1, keepdims=True)
    variance = jnp.mean(centered * centered, axis=-1, keepdims=True)
    return centered * lax.rsqrt(variance + 1e-05) * gain + shift


def exact_gelu(values):
    return jax.nn.gelu(values, approximate=False)


def local(
    tokens,
    lengths,
    w_query,
    w_key,
    w_value,
    w_out,
    conv_taps,
    w_up,
    b_up,
    w_down,
    gain_attn,
    shift_attn,
    gain_ffn,
    shift_ffn,
    grad_out,
):
    tokens_here = tokens[0]
    gathered = lax.all_gather(tokens_here, "head", axis=0, tiled=True)
    seq_total = gathered.shape[0]
    valid_mask, pool_matrix = sequence_masks(lengths[0], seq_total)
    width_local = w_query.shape[1]
    head_local = width_local // HEAD_DIM
    w_joint = jnp.concatenate([w_query, w_key, w_value], axis=1)
    projected = jnp.dot(gathered, w_joint, preferred_element_type=jnp.float32).astype(jnp.bfloat16)

    def split_heads(block):
        return block.astype(jnp.float32).reshape(seq_total, head_local, HEAD_DIM).transpose(1, 0, 2)

    def merge_heads(block):
        return block.transpose(1, 0, 2).reshape(seq_total, width_local)

    def attention(query_heads, key_heads, value_heads, taps):
        return jax.vmap(nystrom_head, in_axes=(0, 0, 0, 0, None, None))(
            query_heads, key_heads, value_heads, taps, valid_mask, pool_matrix
        )

    heads_out, attention_back = jax.vjp(
        attention,
        split_heads(projected[:, :width_local]),
        split_heads(projected[:, width_local : 2 * width_local]),
        split_heads(projected[:, 2 * width_local :]),
        conv_taps,
    )
    context = merge_heads(heads_out).astype(jnp.bfloat16)
    attended = lax.psum_scatter(
        jnp.dot(context, w_out, preferred_element_type=jnp.float32).astype(jnp.bfloat16),
        "head",
        scatter_dimension=0,
        tiled=True,
    ).astype(jnp.float32)
    normed, norm_attn_back = jax.vjp(
        layer_norm, tokens_here.astype(jnp.float32) + attended, gain_attn, shift_attn
    )
    normed_low = normed.astype(jnp.bfloat16)
    normed_all = lax.all_gather(normed_low, "head", axis=0, tiled=True)
    upward = jnp.dot(normed_all, w_up, preferred_element_type=jnp.float32) + b_up
    activated, gelu_back = jax.vjp(exact_gelu, upward)
    hidden = activated.astype(jnp.bfloat16)
    downward = lax.psum_scatter(
        jnp.dot(hidden, w_down, preferred_element_type=jnp.float32).astype(jnp.bfloat16),
        "head",
        scatter_dimension=0,
        tiled=True,
    ).astype(jnp.float32)
    result, norm_ffn_back = jax.vjp(layer_norm, normed + downward, gain_ffn, shift_ffn)
    d_sum, d_gain_ffn, d_shift_ffn = norm_ffn_back(grad_out[0].astype(jnp.float32))
    d_down_low = d_sum.astype(jnp.bfloat16)
    d_down_all = lax.all_gather(d_down_low, "head", axis=0, tiled=True)
    d_w_down = jnp.einsum("tf,td->fd", hidden, d_down_all, preferred_element_type=jnp.float32)
    d_hidden = jnp.einsum("td,fd->tf", d_down_all, w_down, preferred_element_type=jnp.float32)
    d_upward = gelu_back(d_hidden)[0].astype(jnp.bfloat16)
    d_b_up = jnp.sum(d_upward, axis=0, dtype=jnp.float32)
    d_w_up = jnp.einsum("td,tf->df", normed_all, d_upward, preferred_element_type=jnp.float32)
    d_normed = d_sum + lax.psum_scatter(
        jnp.einsum("tf,df->td", d_upward, w_up, preferred_element_type=jnp.float32).astype(
            jnp.bfloat16
        ),
        "head",
        scatter_dimension=0,
        tiled=True,
    ).astype(jnp.float32)
    d_residual, d_gain_attn, d_shift_attn = norm_attn_back(d_normed)
    d_attended_low = d_residual.astype(jnp.bfloat16)
    d_attended_all = lax.all_gather(d_attended_low, "head", axis=0, tiled=True)
    d_w_out = jnp.einsum("tc,td->cd", context, d_attended_all, preferred_element_type=jnp.float32)
    d_context = jnp.einsum("td,cd->tc", d_attended_all, w_out, preferred_element_type=jnp.float32)
    d_heads = d_context.reshape(seq_total, head_local, HEAD_DIM).transpose(1, 0, 2)
    d_query, d_key, d_value, d_conv_taps = attention_back(d_heads)
    d_projected = jnp.concatenate(
        [merge_heads(d_query), merge_heads(d_key), merge_heads(d_value)], axis=1
    ).astype(jnp.bfloat16)
    d_w_joint = jnp.einsum("td,tc->dc", gathered, d_projected, preferred_element_type=jnp.float32)
    d_tokens = d_residual + lax.psum_scatter(
        jnp.einsum("tc,dc->td", d_projected, w_joint, preferred_element_type=jnp.float32).astype(
            jnp.bfloat16
        ),
        "head",
        scatter_dimension=0,
        tiled=True,
    ).astype(jnp.float32)
    d_w_query = d_w_joint[:, :width_local]
    d_w_key = d_w_joint[:, width_local : 2 * width_local]
    d_w_value = d_w_joint[:, 2 * width_local :]
    d_w_query, d_w_key, d_w_value, d_w_out, d_conv_taps, d_w_up, d_b_up, d_w_down = lax.psum(
        (d_w_query, d_w_key, d_w_value, d_w_out, d_conv_taps, d_w_up, d_b_up, d_w_down), "batch"
    )
    d_gain_attn, d_shift_attn, d_gain_ffn, d_shift_ffn = lax.psum(
        (d_gain_attn, d_shift_attn, d_gain_ffn, d_shift_ffn), ("batch", "head")
    )
    return (
        result.astype(jnp.bfloat16)[None],
        d_tokens[None],
        d_w_query,
        d_w_key,
        d_w_value,
        d_w_out,
        d_conv_taps,
        d_w_up,
        d_b_up,
        d_w_down,
        d_gain_attn,
        d_shift_attn,
        d_gain_ffn,
        d_shift_ffn,
    )


def solution(mesh):
    return jax.shard_map(
        local,
        mesh=mesh,
        in_specs=(
            P("batch", "head", None),
            P("batch"),
            P(None, "head"),
            P(None, "head"),
            P(None, "head"),
            P("head", None),
            P("head", None),
            P(None, "head"),
            P("head"),
            P("head", None),
            P(),
            P(),
            P(),
            P(),
            P("batch", "head", None),
        ),
        out_specs=(
            P("batch", "head", None),
            P("batch", "head", None),
            P(None, "head"),
            P(None, "head"),
            P(None, "head"),
            P("head", None),
            P("head", None),
            P(None, "head"),
            P("head"),
            P("head", None),
            P(),
            P(),
            P(),
            P(),
        ),
        check_vma=False,
    )
```

profile of v0, /device:TPU:0, one launch (start us, length us, event | category | flops | bytes accessed | tf_op | source)
XLA Modules:
  0.0 799.1 jit_solution(4572047891264001120)
XLA Ops:
  19.1 21.8 %all-gather.12.cloned.1.call-done = bf16[1,2048,768]{2,1,0:T(8,128)(2,1)} async-done(((bf16[1,512,768]{2,1,0:T(8,128)(2,1)}), bf16[1,2048,768]{2,1,0:T(8,128)(2,1)}) %all-gather.12.cloned.1.call-update) | async-done | bytes 3145744 | tf_op jit(solution)/shard_map/all_gather | solution.py:97
  70.7 28.5 %fusion.25 = bf16[3,2048,64]{1,2,0:T(8,128)(2,1)S(1)} fusion(f32[3,64,64]{2,1,0:T(8,128)S(1)} %fusion.157, bf16[2048,3,64]{0,2,1:T(8,128)(2,1)S(1)} %bitcast.387, f32[3]{0:T(128)} %get-tuple-element.163, f32[3]{0:T(128)} %get-tuple-element.164, f32[3]{0:T(128)S(1)} %get-tuple-element.101, f32[3]{0:T(128)S(1)} %copy-done.119, f32[3]{0:T(128)S(1)} %copy-done.121, ...), kind=kOutput, calls=%fused_computation.42 | convolution fusion | flops 354680832 | bytes 4801292 | tf_op jit(solution)/shard_map/jvp(vmap())/dot_general | solution.py:12
  102.9 38.0 %reduce-scatter.5.cloned.1.call-done = bf16[512,768]{1,0:T(8,128)(2,1)} async-done(((bf16[2048,768]{1,0:T(8,128)(2,1)}), bf16[512,768]{1,0:T(8,128)(2,1)}) %reduce-scatter.5.cloned.1.call-update) | async-done | bytes 786448 | tf_op jit(solution)/shard_map/reduce_scatter | solution.py:124
  146.8 28.6 %all-gather.6.cloned.1.call-done = bf16[2048,768]{1,0:T(8,128)(2,1)} async-done(((bf16[512,768]{1,0:T(8,128)(2,1)}), bf16[2048,768]{1,0:T(8,128)(2,1)}) %all-gather.6.cloned.1.call-update) | async-done | bytes 3145744 | tf_op jit(solution)/shard_map/all_gather | solution.py:134
  175.5 18.6 %multiply_convert_fusion = (bf16[2048,768]{1,0:T(8,128)(2,1)S(1)}, f32[2048,768]{1,0:T(8,128)}, f32[2048,768]{1,0:T(8,128)}) fusion(f32[768]{0:T(1024)S(1)} %copy-done.228, bf16[2048,768]{1,0:T(8,128)(2,1)} %all-gather.6.cloned.1.call-done, bf16[768,768]{1,0:T(8,128)(2,1)S(1)} %copy-done), kind=kOutput, calls=%fused_computation.6 | convolution fusion | flops 2519728128 | bytes 20057088 | tf_op jit(solution)/shard_map/dot_general | solution.py:135
  199.8 38.1 %reduce-scatter.7.cloned.1.call-done = bf16[512,768]{1,0:T(8,128)(2,1)} async-done(((bf16[2048,768]{1,0:T(8,128)(2,1)}), bf16[512,768]{1,0:T(8,128)(2,1)}) %reduce-scatter.7.cloned.1.call-update) | async-done | bytes 786448 | tf_op jit(solution)/shard_map/reduce_scatter | solution.py:138
  247.2 28.6 %all-gather.8.cloned.1.call-done = bf16[2048,768]{1,0:T(8,128)(2,1)} async-done(((bf16[512,768]{1,0:T(8,128)(2,1)}), bf16[2048,768]{1,0:T(8,128)(2,1)}) %all-gather.8.cloned.1.call-update) | async-done | bytes 3145744 | tf_op jit(solution)/shard_map/all_gather | solution.py:147
  275.8 11.1 %convert_reduce_fusion = (f32[768]{0:T(1024)}, bf16[2048,768]{1,0:T(8,128)(2,1)S(1)}) fusion(f32[2048,768]{1,0:T(8,128)} %get-tuple-element.192, f32[2048,768]{1,0:T(8,128)} %get-tuple-element.276, f32[768]{0:T(1024)S(1)} %copy-done.228, bf16[2048,768]{1,0:T(8,128)(2,1)} %all-gather.8.cloned.1.call-done, bf16[768,768]{1,0:T(8,128)(2,1)} %param.24), kind=kOutput, calls=%fused_computation.4 | convolution fusion | flops 2442657024 | bytes 20060160 | tf_op jit(solution)/shard_map/td,fd->tf/dot_general | solution.py:149
  292.7 38.1 %reduce-scatter.9.cloned.1.call-done = bf16[512,768]{1,0:T(8,128)(2,1)} async-done(((bf16[2048,768]{1,0:T(8,128)(2,1)}), bf16[512,768]{1,0:T(8,128)(2,1)}) %reduce-scatter.9.cloned.1.call-update) | async-done | bytes 786448 | tf_op jit(solution)/shard_map/reduce_scatter | solution.py:153
  341.5 25.9 %all-gather.10.cloned.1.call-done = bf16[2048,768]{1,0:T(8,128)(2,1)} async-done(((bf16[512,768]{1,0:T(8,128)(2,1)}), bf16[2048,768]{1,0:T(8,128)(2,1)}) %all-gather.10.cloned.1.call-update) | async-done | bytes 3145744 | tf_op jit(solution)/shard_map/all_gather | solution.py:163
  391.9 9.7 %multiply_reduce_fusion.58 = (f32[3]{0:T(128)}, f32[3]{0:T(128)}, f32[3,2048,64]{1,2,0:T(8,128)}, f32[3,2048,64]{1,2,0:T(8,128)}, f32[3,2048,64]{1,2,0:T(8,128)}...) fusion(f32[3,2048,64]{1,2,0:T(8,128)S(1)} %bitcast.373, ...), kind=kLoop, calls=%fused_computation.134 | loop fusion | flops 7864314 | bytes 25960640 | tf_op jit(solution)/shard_map/transpose(jvp(vmap()))/reduce_sum | solution.py:47
  401.9 8.1 %broadcast_multiply_fusion.2 = (f32[3,2048,64]{1,2,0:T(8,128)}, f32[3,2048,64]{1,2,0:T(8,128)}, f32[3,2048,64]{1,2,0:T(8,128)}, f32[3,2048,64]{1,2,0:T(8,128)}, ...) fusion(f32[3,2048,64]{1,2,0:T(8,128)S(1)} %bitcast.374, ...), kind=kLoop, calls=%fused_computation.240 | loop fusion | flops 5898240 | bytes 25166004 | tf_op jit(solution)/shard_map/transpose(jvp(vmap()))/mul | solution.py:47
  410.2 11.8 %broadcast_multiply_fusion.1 = (f32[3,2048,64]{1,2,0:T(8,128)}, f32[3,2048,64]{1,2,0:T(8,128)}, f32[3,2048,64]{1,2,0:T(8,128)}, f32[3,2048,64]{1,2,0:T(8,128)}, ...) fusion(f32[3,2048,64]{1,2,0:T(8,128)S(1)} %bitcast.375, ...), kind=kLoop, calls=%fused_computation.239 | loop fusion | flops 7077888 | bytes 29884632 | tf_op jit(solution)/shard_map/transpose(jvp(vmap()))/mul | solution.py:47
  422.1 12.0 %broadcast_multiply_fusion = (f32[3,2048,64]{1,2,0:T(8,128)}, f32[3,2048,64]{1,2,0:T(8,128)}, f32[3,2048,64]{1,2,0:T(8,128)}, f32[3,2048,64]{1,2,0:T(8,128)}, f3...) fusion(f32[3,2048,64]{1,2,0:T(8,128)S(1)} %bitcast.376, ...), kind=kLoop, calls=%fused_computation.238 | loop fusion | flops 7077888 | bytes 29884632 | tf_op jit(solution)/shard_map/transpose(jvp(vmap()))/mul | solution.py:47
  451.1 35.9 %pad_add_fusion = f32[3,2112,64]{1,2,0:T(8,128)} fusion(f32[3,2048,64]{1,2,0:T(8,128)} %get-tuple-element.206, f32[3,2048,64]{1,2,0:T(8,128)} %get-tuple-element.207, f32[3,2048,64]{1,2,0:T(8,128)} %get-tuple-element.208, f32[3,2048,64]{1,2,0:T(8,128)} %get-tuple-element.209, f32[3,2048,64]{1,2,0:T(8,128)} %get-tuple-element.210, ...), kind=kLoop, calls=%fused_computation.55 | loop fusion | flops 23519232 | bytes 94420992 | tf_op jit(solution)/shard_map/transpose(jvp(vmap()))/add_any | solution.py:47
  487.0 8.1 %fusion.26 = bf16[3,2048,64]{1,2,0:T(8,128)(2,1)S(1)} fusion(f32[3,64,64]{2,1,0:T(8,128)S(1)} %copy-done.43, f32[3,2048,64]{1,2,0:T(8,128)} %get-tuple-element.200, f32[3,2048,64]{1,2,0:T(8,128)} %get-tuple-element.201, f32[3,2048,64]{1,2,0:T(8,128)} %get-tuple-element.202, f32[3,2048,64]{1,2,0:T(8,128)} %get-tuple-element.203, ...), kind=kOutput, calls=%fused_computation.43 | convolution fusion | flops 306315264 | bytes 13428224 | tf_op jit(solution)/shard_map/transpose(jvp(vmap()))/dot_general | solution.py:12
  496.0 4.2 convolution_convert_fusion.2
  500.6 7.1 fusion.175
  507.7 4.2 fusion.174
  519.6 40.3 %all-reduce.131 = (f32[768]{0:T(1024)}, f32[768]{0:T(1024)}, f32[768]{0:T(1024)}, f32[768]{0:T(1024)}) all-reduce(f32[768]{0:T(1024)S(1)} %copy-done.103, f32[768]{0:T(1024)S(1)} %copy-done.104, f32[768]{0:T(1024)S(1)} %copy-done.102, f32[768]{0:T(1024)S(1)} %convert_reduce_fusion.1), channel_id=1, replica_groups=mesh['batch'=8,'head'=4] {'batch','head'}, use_global_device_ids=true, to_apply=%region_103.104 | all-reduce | flops 3072 | bytes 24576 | tf_op jit(solution)/shard_map/psum | solution.py:186
  580.0 4.1 multiply_reduce_fusion.62
  584.1 4.3 multiply_reduce_fusion.63
  588.6 40.6 %all-reduce.132 = (f32[3,65]{0,1:T(8,128)S(1)}, f32[768]{0:T(1024)}) all-reduce(f32[3,65]{0,1:T(8,128)S(1)} %pad_add_fusion.7, f32[768]{0:T(1024)S(1)} %copy-done.116), channel_id=1, replica_groups=mesh['batch'=8,'head'=4] {'batch'}, use_global_device_ids=true, to_apply=%region_97.98 | all-reduce | flops 963 | bytes 7704 | tf_op jit(solution)/shard_map/psum | solution.py:183
  632.9 151.0 %all-reduce.136.cloned.1.call-done = (f32[768,192]{0,1:T(8,128)}, f32[768,192]{0,1:T(8,128)}, f32[768,192]{0,1:T(8,128)}, f32[192,768]{1,0:T(8,128)}, f32[768,768]{1,0:T(8,128)}, /*index=5*/f32[768,768]{1,0:T(8,128)}) async-done(((f32[768,192]{0,1:T(8,128)}, f32[768,192]{0,1:T(8,128)}, f32[768,192]{0,1:T(8,128)}, f32[192,768]{1,0:T(8,128)}, f32[768,768]{1,0:T(8,128)}, /*index=5*/f32[768,768]{1,0:T(8,128)}), ...) | async-done | bytes 7077904 | tf_op jit(solution)/shard_map/psum | solution.py:183
  (657 shorter events, 162.0 us)
Async XLA Ops:
  7.2 168.3 %copy-start = (bf16[768,768]{1,0:T(8,128)(2,1)S(1)}, bf16[768,768]{1,0:T(8,128)(2,1)}, u32[]{:S(2)}) copy-start(bf16[768,768]{1,0:T(8,128)(2,1)} %param.22) | copy-start | bytes 3538948
  7.2 33.7 %all-gather.12.cloned.1.call-start = ((), (), s32[]{:S(2)}) async-start(), calls=%async_computation.11 | async-start | bytes 3932160 | tf_op jit(solution)/shard_map/all_gather | solution.py:97
  8.0 133.0 %reduce-scatter.5.cloned.1.call-start = ((), (), s32[]{:S(2)}) async-start(), calls=%async_computation.4 | async-start | bytes 3932160 | tf_op jit(solution)/shard_map/reduce_scatter | solution.py:124
  8.7 55.8 %copy-start.93 = (f32[2048]{0:T(1024)}, f32[2048]{0:T(1024)S(1)}, u32[]{:S(2)}) copy-start(f32[2048]{0:T(1024)S(1)} %fusion.130) | copy-start | bytes 24580
  8.7 55.8 %copy-start.107 = (pred[2048]{0:T(1024)(128)(4,1)}, pred[2048]{0:T(1024)(128)(4,1)S(1)}, u32[]{:S(2)}) copy-start(pred[2048]{0:T(1024)(128)(4,1)S(1)} %get-tuple-element.286) | copy-start | bytes 6148
  15.4 54.9 %copy-start.117 = (f32[3]{0:T(128)}, f32[3]{0:T(128)S(1)}, u32[]{:S(2)}) copy-start(f32[3]{0:T(128)S(1)} %get-tuple-element.101) | copy-start | bytes 40
  19.1 28.4 %copy-start.216 = (s32[64]{0:T(128)}, s32[64]{0:T(128)S(1)}, u32[]{:S(2)}) copy-start(s32[64]{0:T(128)S(1)} %get-tuple-element.267) | copy-start | bytes 772
  19.1 28.4 %copy-start.218 = (f32[64]{0:T(128)}, f32[64]{0:T(128)S(1)}, u32[]{:S(2)}) copy-start(f32[64]{0:T(128)S(1)} %get-tuple-element.268) | copy-start | bytes 772
  19.1 28.4 %copy-start.220 = (s32[64]{0:T(128)}, s32[64]{0:T(128)S(1)}, u32[]{:S(2)}) copy-start(s32[64]{0:T(128)S(1)} %get-tuple-element.269) | copy-start | bytes 772
  69.9 29.3 %copy-start.85 = (f32[3,64,64]{2,1,0:T(8,128)}, f32[3,64,64]{2,1,0:T(8,128)S(1)}, u32[]{:S(2)}) copy-start(f32[3,64,64]{2,1,0:T(8,128)S(1)} %fusion.157) | copy-start | bytes 147460
  70.7 29.4 %copy-start.42 = (bf16[192,768]{1,0:T(8,128)(2,1)S(1)}, bf16[192,768]{1,0:T(8,128)(2,1)}, u32[]{:S(2)}) copy-start(bf16[192,768]{1,0:T(8,128)(2,1)} %param.20) | copy-start | bytes 884740
  102.9 41.4 %copy-start.95 = (f32[768]{0:T(1024)S(1)}, f32[768]{0:T(1024)}, u32[]{:S(2)}) copy-start(f32[768]{0:T(1024)} %param.25) | copy-start | bytes 9220
  102.9 41.4 %copy-start.105 = (f32[768]{0:T(1024)S(1)}, f32[768]{0:T(1024)}, u32[]{:S(2)}) copy-start(f32[768]{0:T(1024)} %param.26) | copy-start | bytes 9220
  102.9 72.6 %all-gather.6.cloned.1.call-start = ((), (), s32[]{:S(2)}) async-start(), calls=%async_computation.5 | async-start | bytes 3932160 | tf_op jit(solution)/shard_map/all_gather | solution.py:134
  144.3 31.2 %copy-start.228 = (f32[768]{0:T(1024)S(1)}, f32[768]{0:T(1024)}, u32[]{:S(2)}) copy-start(f32[768]{0:T(1024)} %param.23) | copy-start | bytes 9220
  146.8 91.1 %reduce-scatter.7.cloned.1.call-start = ((), (), s32[]{:S(2)}) async-start(), calls=%async_computation.6 | async-start | bytes 3932160 | tf_op jit(solution)/shard_map/reduce_scatter | solution.py:138
  199.7 76.1 %all-gather.8.cloned.1.call-start = ((), (), s32[]{:S(2)}) async-start(), calls=%async_computation.7 | async-start | bytes 3932160 | tf_op jit(solution)/shard_map/all_gather | solution.py:147
  247.1 83.6 %reduce-scatter.9.cloned.1.call-start = ((), (), s32[]{:S(2)}) async-start(), calls=%async_computation.8 | async-start | bytes 3932160 | tf_op jit(solution)/shard_map/reduce_scatter | solution.py:153
  292.6 38.1 %copy-start.2 = (bf16[1,512,768]{2,1,0:T(8,128)(2,1)S(1)}, bf16[1,512,768]{2,1,0:T(8,128)(2,1)}, u32[]{:S(2)}) copy-start(bf16[1,512,768]{2,1,0:T(8,128)(2,1)} %param.15) | copy-start | bytes 2359300
  292.6 38.1 %copy-start.4 = (bf16[512,768]{1,0:T(8,128)(2,1)S(1)}, bf16[512,768]{1,0:T(8,128)(2,1)}, u32[]{:S(2)}) copy-start(bf16[512,768]{1,0:T(8,128)(2,1)} %reduce-scatter.5.cloned.1.call-done) | copy-start | bytes 2359300
  292.6 74.7 %all-gather.10.cloned.1.call-start = ((), (), s32[]{:S(2)}) async-start(), calls=%async_computation.9 | async-start | bytes 3932160 | tf_op jit(solution)/shard_map/all_gather | solution.py:163
  338.7 291.2 %reduce-scatter.11.cloned.1.call-start = ((), (), s32[]{:S(2)}) async-start(), calls=%async_computation.10 | async-start | bytes 3932160 | tf_op jit(solution)/shard_map/reduce_scatter | solution.py:172
  500.2 283.7 %all-reduce.136.cloned.1.call-start = ((), (), s32[]{:S(2)}) async-start(), calls=%async_computation.12 | async-start | bytes 14155776 | tf_op jit(solution)/shard_map/psum | solution.py:183
  584.1 45.8 %copy-start.97 = (f32[512]{0:T(512)S(1)}, f32[512]{0:T(512)}, u32[]{:S(2)}) copy-start(f32[512]{0:T(512)} %copy-done.96) | copy-start | bytes 6148
  (221 other events, 976.3 us)
Sparse Core Ops, SparseCore 0:
  9.6 31.2 all-gather.11
  103.0 37.9 reduce-scatter.4
  146.9 28.5 all-gather.5
  199.9 37.9 reduce-scatter.6
  247.3 28.5 all-gather.7
  292.8 37.9 reduce-scatter.8
  338.8 28.5 all-gather.9
  500.3 38.6 reduce-scatter.10
  545.2 238.6 all-reduce.135
where the time goes:
time: 806 us; the launch traced here: 799 us
  waiting for transfers between devices  371 us (46%)
  matrix products  155 us (19%)
  other arithmetic  138 us (17%)
  blocking collectives  80.9 us (10%)
  local copies, waits for them, and re-layouts  34.5 us (4%)
  between operations  18.6 us (2%)
    psum x1, waiting for transfers between devices, local(): lax.psum((d_w_query, d_w_key, d_w_value, d_w_out, d_conv_taps, d_w_up, d_...  151 us
    dot_general x92, matrix products, matmul(): return jnp.dot(left, right, precision=lax.Precision.HIGHEST)  85.1 us
    psum x1, blocking collectives, local(): lax.psum((d_w_query, d_w_key, d_w_value, d_w_out, d_conv_taps, d_w_up, d_...  40.6 us
    psum x1, blocking collectives, local(): lax.psum((d_gain_attn, d_shift_attn, d_gain_ffn, d_shift_ffn), ('batch',...  40.3 us
    reduce_sum x8, other arithmetic, depthwise(): summed = summed + taps[offset] * padded[offset:offset + row_total]  38.2 us
    reduce_scatter x1, waiting for transfers between devices, local(): lax.psum_scatter(jnp.einsum('tf,df->td', d_upward, w_up, preferred_elemen...  38.1 us
    reduce_scatter x1, waiting for transfers between devices, local(): lax.psum_scatter(jnp.dot(hidden, w_down, preferred_element_type=jnp.float...  38.1 us
    reduce_scatter x1, waiting for transfers between devices, local(): lax.psum_scatter(jnp.dot(context, w_out, preferred_element_type=jnp.float...  38 us
  transfers between devices with their start and end apart: 9, of which 8 were waited for; matrix products, arithmetic and copies ran while one was open for 8% of the time, Pallas kernels for 0%

commit v1 on v0

v1 whole, which is shorter than its diff:
```python
import functools

import jax
import jax.numpy as jnp
from jax import lax
from jax.experimental import pallas as pl
from jax.experimental.pallas import tpu as pltpu
from jax.sharding import PartitionSpec as P

f32 = jnp.float32
bf16 = jnp.bfloat16
HEAD_DIM = 64
LANDMARKS = 64
NEWTON = 6
TAPS = 65
HALO = TAPS // 2
GROUP = 256
NN = ((1,), (0,))
NT = ((1,), (1,))
TN = ((0,), (0,))
VMEM = pltpu.VMEM
ANY = pl.ANY


def dot(a, b, dims=NN):
    return lax.dot_general(a, b, (dims, ((), ())), preferred_element_type=f32)


def split(x):
    high = x.astype(bf16)
    return high, (x - high.astype(f32)).astype(bf16)


def mm(a, b, dims=NN):
    a_high, a_low = split(a)
    b_high, b_low = split(b)
    return dot(a_high, b_high, dims) + (dot(a_high, b_low, dims) + dot(a_low, b_high, dims))


def mm_left(a, b, dims=NN):
    a_high, a_low = split(a)
    return dot(a_high, b, dims) + dot(a_low, b, dims)


def iota(shape, dim):
    return lax.broadcasted_iota(jnp.int32, shape, dim)


def call(body, outs, ins, scratch=(), flops=0, size=0, limit=40, name=None, smem=()):
    specs = [
        pl.BlockSpec(memory_space=pltpu.SMEM) if i in smem else pl.BlockSpec(memory_space=space)
        for i, (space, _) in enumerate(ins)
    ]
    return pl.pallas_call(
        body,
        out_shape=[jax.ShapeDtypeStruct(s, d) for s, d in outs],
        in_specs=specs,
        out_specs=[pl.BlockSpec(memory_space=VMEM)] * len(outs),
        scratch_shapes=list(scratch),
        compiler_params=pltpu.CompilerParams(vmem_limit_bytes=limit << 20),
        cost_estimate=pl.CostEstimate(flops=flops, bytes_accessed=size, transcendentals=0),
        name=name,
    )(*[value for _, value in ins])


def block_mask():
    return (iota((GROUP, GROUP), 0) >> 6) == (iota((GROUP, GROUP), 1) >> 6)


def spread(x):
    return jnp.where(block_mask(), jnp.concatenate([x, x, x, x], axis=0), 0.0)


def fold(x):
    kept = jnp.where(block_mask(), x, 0.0)
    return kept[0:64] + kept[64:128] + kept[128:192]


def rows_of(info, count, first):
    return info[1] + first + iota((count, 1), 0)


def landmark_kernel(p0, p1, p2, p3, wt, lm, chain):
    pooled = p0[...] + p1[...] + p2[...] + p3[...]
    high, low = split(pooled)
    both = jnp.concatenate([high, low], axis=0)
    lm[...] = jnp.zeros_like(lm)
    matrices, starts = [], []
    for head in range(3):
        pair = []
        for kind in range(2):
            rows = wt[kind * 192 + head * 64 : kind * 192 + head * 64 + 64]
            out = dot(both, rows, NT)
            out = out[0:64] + out[64:128]
            lm[:, kind * GROUP + head * 64 : kind * GROUP + head * 64 + 64] = out
            pair.append(out)
        scores = mm(pair[0], pair[1], NT) * 0.125
        raised = jnp.exp(scores - jnp.max(scores, axis=1, keepdims=True))
        matrix = raised / jnp.sum(raised, axis=1, keepdims=True)
        column = jnp.max(jnp.sum(matrix, axis=0, keepdims=True), axis=1, keepdims=True)
        row = jnp.max(jnp.sum(matrix, axis=1, keepdims=True), axis=0, keepdims=True)
        matrices.append(matrix)
        starts.append(matrix.T / (column * row))
    eye = (iota((64, 64), 0) == iota((64, 64), 1)).astype(f32)

    def step(it, iterates):
        results = []
        for head in range(3):
            z = iterates[head]
            product = mm(matrices[head], z)
            inner1 = 7.0 * eye - product
            inner2 = 15.0 * eye - mm(product, inner1)
            inner3 = 13.0 * eye - mm(product, inner2)
            chain[it, 0, head] = z
            chain[it, 1, head] = product
            chain[it, 2, head] = inner2
            chain[it, 3, head] = inner3
            results.append(0.25 * mm(z, inner3))
        return tuple(results)

    finals = lax.fori_loop(0, NEWTON, step, tuple(starts))
    for head in range(3):
        lm[:, 2 * GROUP + head * 64 : 2 * GROUP + head * 64 + 64] = finals[head]


def inverse_back_kernel(x0, x1, x2, x3, wst, lm, chain, out):
    total = x0[...] + x1[...] + x2[...] + x3[...]
    eye = (iota((64, 64), 0) == iota((64, 64), 1)).astype(f32)
    weight = wst[...]
    out[...] = jnp.zeros_like(out)
    grads, matrices, queries, keys = [], [], [], []
    for head in range(3):
        at = slice(head * 64, head * 64 + 64)
        grads.append(mm(total[:, at], weight[:, at], NT))
        query = lm[:, head * 64 : head * 64 + 64]
        key = lm[:, GROUP + head * 64 : GROUP + head * 64 + 64]
        scores = mm(query, key, NT) * 0.125
        raised = jnp.exp(scores - jnp.max(scores, axis=1, keepdims=True))
        matrices.append(raised / jnp.sum(raised, axis=1, keepdims=True))
        queries.append(query)
        keys.append(key)

    def step(count, carried):
        it = NEWTON - 1 - count
        results = []
        for head in range(3):
            dz_next, da = carried[2 * head], carried[2 * head + 1]
            z = chain[it, 0, head]
            product = chain[it, 1, head]
            inner1 = 7.0 * eye - product
            inner2 = chain[it, 2, head]
            inner3 = chain[it, 3, head]
            dz_next = 0.25 * dz_next
            dz = mm(dz_next, inner3, NT)
            d3 = -mm(z, dz_next, TN)
            d2 = -mm(product, d3, TN)
            d1 = mm(product, d2, TN)
            dp = mm(d3, inner2, NT) + mm(d2, inner1, NT) - d1
            da = da + mm(dp, z, NT)
            dz = dz + mm(matrices[head], dp, TN)
            results += [dz, da]
        return tuple(results)

    first = []
    for head in range(3):
        first += [grads[head], jnp.zeros((64, 64), f32)]
    last = lax.fori_loop(0, NEWTON, step, tuple(first))
    for head in range(3):
        dz, da = last[2 * head], last[2 * head + 1]
        matrix = matrices[head]
        columns = jnp.sum(matrix, axis=0, keepdims=True)
        rows = jnp.sum(matrix, axis=1, keepdims=True)
        column = jnp.max(columns, axis=1, keepdims=True)
        row = jnp.max(rows, axis=0, keepdims=True)
        scale = 1.0 / (column * row)
        da = da + dz.T * scale
        d_scale = -jnp.sum(jnp.sum(dz * matrix.T, axis=1, keepdims=True), axis=0, keepdims=True) * scale * scale
        column_hit = (columns == column).astype(f32)
        row_hit = (rows == row).astype(f32)
        da = da + d_scale * row * column_hit / jnp.sum(column_hit, axis=1, keepdims=True)
        da = da + d_scale * column * row_hit / jnp.sum(row_hit, axis=0, keepdims=True)
        ds = matrix * (da - jnp.sum(da * matrix, axis=1, keepdims=True)) * 0.125
        out[:, head * 64 : head * 64 + 64] = mm(ds, keys[head])
        out[:, GROUP + head * 64 : GROUP + head * 64 + 64] = mm(ds, queries[head], TN)


def fetch_projection(weights, held, sems):
    for i in range(4):
        for kind in range(3):
            pltpu.make_async_copy(
                weights[i].at[pl.ds(kind * 192, 192)], held.at[i, pl.ds(kind * GROUP, 192)], sems.at[i, kind]
            ).start()
            held[i, kind * GROUP + 192 : kind * GROUP + 256, :] = jnp.zeros((64, held.shape[2]), bf16)


def await_projection(weights, held, sems, i):
    for kind in range(3):
        pltpu.make_async_copy(
            weights[0].at[pl.ds(kind * 192, 192)], held.at[i, pl.ds(kind * GROUP, 192)], sems.at[i, kind]
        ).wait()


def project_kernel(info, tokens, before, after, w0, w1, w2, w3, q_out, k_out, v_out, held, sems):
    count = tokens.shape[0]
    fetch_projection((w0, w1, w2, w3), held, sems)
    valid = (rows_of(info, count, 0) < info[0]).astype(f32)
    valid_before = (rows_of(info, HALO, -HALO) < info[0]).astype(f32)
    valid_after = (rows_of(info, HALO, count) < info[0]).astype(f32)

    def body(i, _):
        await_projection((w0, w1, w2, w3), held, sems, i)
        for kind, out in ((0, q_out), (1, k_out)):
            out[i] = (dot(tokens[...], held[i, kind * GROUP : kind * GROUP + GROUP], NT) * valid).astype(bf16)
        wv = held[i, 2 * GROUP : 3 * GROUP]
        v_out[i, HALO : HALO + count] = (dot(tokens[...], wv, NT) * valid).astype(bf16)
        v_out[i, 0:HALO] = (dot(before[...], wv, NT) * valid_before).astype(bf16)
        v_out[i, HALO + count : 2 * HALO + count] = (dot(after[...], wv, NT) * valid_after).astype(bf16)
        v_out[i, 2 * HALO + count :] = jnp.zeros((v_out.shape[1] - 2 * HALO - count, GROUP), bf16)
        return 0

    lax.fori_loop(0, 4, body, 0)


def third_scores(info, lm, k_ref, i):
    count = k_ref.shape[1]
    valid = info[1] + iota((1, count), 1) < info[0]
    queries = spread(lm[i, :, 0:GROUP])
    return jnp.where(valid, mm_left(queries, k_ref[i], NT) * 0.125, -1e30)


def third_kernel(info, lm, k_ref, v_ref, pay):
    count = k_ref.shape[1]
    lane = iota((64, GROUP), 1)

    def body(i, _):
        scores = third_scores(info, lm, k_ref, i)
        top = jnp.max(scores, axis=1, keepdims=True)
        raised = jnp.exp(scores - top)
        total = jnp.sum(raised, axis=1, keepdims=True)
        packed = fold(mm_left(raised, v_ref[i, HALO : HALO + count]))
        for head in range(3):
            packed = jnp.where(lane == 192 + head, top[head * 64 : head * 64 + 64], packed)
            packed = jnp.where(lane == 196 + head, total[head * 64 : head * 64 + 64], packed)
        pay[i] = packed
        return 0

    lax.fori_loop(0, 4, body, 0)


def first_scores(lm, q_ref, i):
    keys = spread(lm[i, :, GROUP : 2 * GROUP])
    count = q_ref.shape[1]
    scores = (mm_left(keys, q_ref[i], NT) * 0.125).reshape(4, 64, count)
    raised = jnp.exp(scores - jnp.max(scores, axis=1, keepdims=True))
    return raised / jnp.sum(raised, axis=1, keepdims=True)


def toeplitz(row):
    return pltpu.roll(jnp.broadcast_to(row, (128, GROUP)), 0, 1, stride=1, stride_axis=0)


def head_select(x, rows):
    lane = iota((rows, GROUP), 1) >> 6
    out = jnp.where(lane == 0, x[0:rows], 0.0)
    out = jnp.where(lane == 1, x[rows : 2 * rows], out)
    return jnp.where(lane == 2, x[2 * rows : 3 * rows], out)


def context_kernel(p0, p1, p2, p3, lm, q_ref, v_ref, small, ctx, wst, x_out):
    count = q_ref.shape[1]
    lane = iota((64, GROUP), 1)

    def body(i, _):
        parts = [p0[i], p1[i ^ 1], p2[i ^ 2], p3[i ^ 3]]
        factors = [jnp.zeros((64, GROUP), f32) for _ in range(4)]
        stats = jnp.zeros((64, GROUP), f32)
        for head in range(3):
            tops = [part[:, 192 + head : 193 + head] for part in parts]
            top = jnp.maximum(jnp.maximum(tops[0], tops[1]), jnp.maximum(tops[2], tops[3]))
            scales = [jnp.exp(t - top) for t in tops]
            total = sum(part[:, 196 + head : 197 + head] * s for part, s in zip(parts, scales))
            mine = (lane >> 6) == head
            factors = [jnp.where(mine, s / total, f) for s, f in zip(scales, factors)]
            stats = jnp.where(lane == 192 + head, top, stats)
            stats = jnp.where(lane == 196 + head, total, stats)
        weight = sum(part * f for part, f in zip(parts, factors))
        wst[i] = jnp.where(lane < 192, weight, stats)
        mixed = mm(spread(lm[i, :, 2 * GROUP : 3 * GROUP]), spread(weight))
        x_out[i] = fold(mixed)
        first = first_scores(lm, q_ref, i).reshape(GROUP, count)
        main = mm(first, mixed, TN)
        bands = [toeplitz(small[i, 1 + head : 2 + head, 0:GROUP]) for head in range(3)]
        high, low = split(jnp.concatenate(bands, axis=0))
        for block in range(count // 128):
            window = v_ref[i, block * 128 : block * 128 + 256]
            conv = dot(high, window) + dot(low, window)
            ctx[i, block * 128 : block * 128 + 128] = (
                main[block * 128 : block * 128 + 128] + head_select(conv, 128)
            ).astype(bf16)
        return 0

    lax.fori_loop(0, 4, body, 0)


def first_back_kernel(
    g_ref, before, after, o0, o1, o2, o3, lm, q_ref, v_ref, small, x_in, dx, dq, dkl, dv, dtaps, held, sems, ext, dctx
):
    count = g_ref.shape[0]
    width = g_ref.shape[1]
    weights = (o0, o1, o2, o3)
    for i in range(4):
        pltpu.make_async_copy(weights[i], held.at[i, pl.ds(0, 192)], sems.at[i]).start()
        held[i, 192:256, :] = jnp.zeros((64, width), bf16)
    ext[0:HALO] = before[...]
    ext[HALO : HALO + count] = g_ref[...]
    ext[HALO + count : 2 * HALO + count] = after[...]
    ext[2 * HALO + count :] = jnp.zeros((ext.shape[0] - 2 * HALO - count, width), bf16)
    lane = iota((128, GROUP), 1) >> 6
    flip = (iota((128, 128), 0) + iota((128, 128), 1) == 127).astype(bf16)

    def body(i, _):
        pltpu.make_async_copy(weights[0], held.at[i, pl.ds(0, 192)], sems.at[i]).wait()
        dctx[...] = dot(ext[...], held[i], NT)
        own = dctx[HALO : HALO + count]
        own_high, own_low = split(own)
        first = first_scores(lm, q_ref, i)
        flat = first.reshape(GROUP, count)
        flat_high, flat_low = split(flat)
        dx[i] = fold(dot(flat_high, own_high) + (dot(flat_high, own_low) + dot(flat_low, own_high)))
        x_high, x_low = split(spread(x_in[i]))
        dfirst = dot(x_high, own_high, NT) + (dot(x_high, own_low, NT) + dot(x_low, own_high, NT))
        dfirst = dfirst.reshape(4, 64, count)
        ds = first * (dfirst - jnp.sum(first * dfirst, axis=1, keepdims=True)) * 0.125
        ds_high, ds_low = split(ds.reshape(GROUP, count))
        keys_high, keys_low = split(spread(lm[i, :, GROUP : 2 * GROUP]))
        dq[i] = dot(ds_high, keys_high, TN) + (dot(ds_high, keys_low, TN) + dot(ds_low, keys_high, TN))
        dkl[i] = fold(dot(ds_high, q_ref[i]) + dot(ds_low, q_ref[i]))
        bands = [toeplitz(small[i, 4 + head : 5 + head, 0:GROUP]) for head in range(3)]
        high, low = split(jnp.concatenate(bands, axis=0))
        gram = jnp.zeros((384, GROUP), f32)
        for block in range(count // 128):
            window_high, window_low = split(dctx[block * 128 : block * 128 + 256])
            conv = dot(high, window_high) + (dot(high, window_low) + dot(low, window_high))
            dv[i, block * 128 : block * 128 + 128] = head_select(conv, 128)
            piece = dctx[HALO + block * 128 : HALO + block * 128 + 128]
            stacked = jnp.concatenate([jnp.where(lane == head, piece, 0.0) for head in range(3)], axis=0)
            gram = gram + mm_left(stacked, v_ref[i, block * 128 : block * 128 + 256], NT)
        dtaps[i] = jnp.zeros((8, GROUP), f32)
        for head in range(3):
            part_high, part_low = split(gram[head * 128 : head * 128 + 128])
            upturned = dot(flip, part_high) + dot(flip, part_low)
            straight = pltpu.roll(upturned, GROUP - 127, 1, stride=1, stride_axis=0)
            summed = jnp.sum(straight, axis=0, keepdims=True)
            dtaps[i, 1 + head : 2 + head, :] = jnp.where(iota((1, GROUP), 1) < TAPS, summed, 0.0)
        return 0

    lax.fori_loop(0, 4, body, 0)


def third_back_kernel(info, x0, x1, x2, x3, lm, wst, k_ref, v_ref, dvc, dk, dql, dv):
    count = k_ref.shape[1]
    valid = (rows_of(info, count, 0) < info[0]).astype(f32)
    none = jnp.zeros((64, 1), f32)

    def body(i, _):
        dx = spread(x0[i] + x1[i ^ 1] + x2[i ^ 2] + x3[i ^ 3])
        dweight = mm(spread(lm[i, :, 2 * GROUP : 3 * GROUP]), dx, TN)
        stats = wst[i]
        weight = spread(jnp.where(iota((64, GROUP), 1) < 192, stats, 0.0))
        inner = jnp.sum(dweight * weight, axis=1, keepdims=True)
        top = jnp.concatenate([stats[:, 192 + head : 193 + head] for head in range(3)] + [none], axis=0)
        total = jnp.concatenate([stats[:, 196 + head : 197 + head] for head in range(3)] + [none + 1.0], axis=0)
        scores = third_scores(info, lm, k_ref, i)
        third = jnp.exp(scores - top) / total
        dw_high, dw_low = split(dweight)
        values = v_ref[i, HALO : HALO + count]
        dthird = dot(dw_high, values, NT) + dot(dw_low, values, NT)
        ds_high, ds_low = split(third * (dthird - inner) * 0.125)
        queries_high, queries_low = split(spread(lm[i, :, 0:GROUP]))
        dk[i] = dot(ds_high, queries_high, TN) + (dot(ds_high, queries_low, TN) + dot(ds_low, queries_high, TN))
        dql[i] = fold(dot(ds_high, k_ref[i]) + dot(ds_low, k_ref[i]))
        third_high, third_low = split(third)
        dvalues = dot(third_high, dw_high, TN) + (dot(third_high, dw_low, TN) + dot(third_low, dw_high, TN))
        dv[i] = ((dvalues + dvc[i]) * valid).astype(bf16)
        return 0

    lax.fori_loop(0, 4, body, 0)


def joint_back_kernel(info, l0, l1, dq, dk, dv, out):
    count = dq.shape[1]
    mark = iota((1, 64), 1)
    low = (mark * info[0]) >> 6
    high = ((mark + 1) * info[0]) >> 6
    pos = rows_of(info, count, 0)
    member = ((pos >= low) & (pos < high)).astype(bf16)
    member = jnp.concatenate([member, member], axis=1)
    valid = (pos < info[0]).astype(f32)
    row = iota((64, 1), 0)
    width = ((((row + 1) * info[0]) >> 6) - ((row * info[0]) >> 6)).astype(f32)

    def body(i, _):
        pooled = (l0[i].astype(f32) + l1[i ^ 1].astype(f32)) / width
        pooled_high, pooled_low = split(pooled)
        spreads = dot(member, jnp.concatenate([pooled_high, pooled_low], axis=0))
        out[i, :, 0:GROUP] = (dq[i] * valid + spreads[:, 0:GROUP]).astype(bf16)
        out[i, :, GROUP : 2 * GROUP] = (dk[i] * valid + spreads[:, GROUP : 2 * GROUP]).astype(bf16)
        out[i, :, 2 * GROUP : 3 * GROUP] = dv[i]
        return 0

    lax.fori_loop(0, 4, body, 0)


def token_back_kernel(joint, dres, w0, w1, w2, w3, out, held, sems):
    fetch_projection((w0, w1, w2, w3), held, sems)
    out[...] = dres[...]

    def body(i, _):
        await_projection((w0, w1, w2, w3), held, sems, i)
        out[...] += dot(joint[i], held[i])
        return 0

    lax.fori_loop(0, 4, body, 0)


def fetch_all(weights, held, sems):
    for i in range(4):
        pltpu.make_async_copy(weights[i], held.at[i], sems.at[i]).start()


def await_one(weights, held, sems, i):
    pltpu.make_async_copy(weights[0], held.at[i], sems.at[i]).wait()


def moments(x):
    centered = x - jnp.mean(x, axis=-1, keepdims=True)
    variance = jnp.mean(centered * centered, axis=-1, keepdims=True)
    inverse = lax.rsqrt(variance + 1e-05)
    return centered * inverse, inverse


def attended_kernel(ctx, tokens, gain, shift, o0, o1, o2, o3, pre, normed, low, held, sems):
    width = tokens.shape[1]
    weights = (o0, o1, o2, o3)
    for i in range(4):
        pltpu.make_async_copy(weights[i], held.at[i, pl.ds(0, 192)], sems.at[i]).start()
        held[i, 192:256, :] = jnp.zeros((64, width), bf16)
    pre[...] = tokens[...].astype(f32)

    def body(i, _):
        pltpu.make_async_copy(weights[0], held.at[i, pl.ds(0, 192)], sems.at[i]).wait()
        pre[...] += dot(ctx[i], held[i])
        return 0

    lax.fori_loop(0, 4, body, 0)
    unit, _ = moments(pre[...])
    result = unit * gain[...] + shift[...]
    normed[...] = result
    low[...] = result.astype(bf16)


def gelu_parts(u):
    cdf = 0.5 + 0.5 * lax.erf(u * 0.7071067811865476)
    pdf = jnp.exp(u * u * -0.5) * 0.3989422804014327
    return u * cdf, cdf + u * pdf


def up_kernel(low, small, w0, w1, w2, w3, hidden, slope, held, sems):
    fetch_all((w0, w1, w2, w3), held, sems)

    def body(i, _):
        await_one((w0, w1, w2, w3), held, sems, i)
        for chunk in range(3):
            at = slice(chunk * 256, chunk * 256 + 256)
            upward = dot(low[...], held[i, :, at]) + small[i, 0:1, at]
            value, derivative = gelu_parts(upward)
            hidden[i, :, at] = value.astype(bf16)
            slope[i, :, at] = derivative.astype(bf16)
        return 0

    lax.fori_loop(0, 4, body, 0)


def norm_back(g, gain, unit, inverse):
    scaled = g * gain
    mean1 = jnp.mean(scaled, axis=-1, keepdims=True)
    mean2 = jnp.mean(scaled * unit, axis=-1, keepdims=True)
    return (scaled - mean1 - unit * mean2) * inverse


def down_kernel(hidden, normed, grad, gain, shift, w0, w1, w2, w3, out, dsum, dlow, sums, held, sems, acc):
    fetch_all((w0, w1, w2, w3), held, sems)
    acc[...] = normed[...]

    def body(i, _):
        await_one((w0, w1, w2, w3), held, sems, i)
        acc[...] += dot(hidden[i], held[i])
        return 0

    lax.fori_loop(0, 4, body, 0)
    unit, inverse = moments(acc[...])
    out[...] = (unit * gain[...] + shift[...]).astype(bf16)
    g = grad[...].astype(f32)
    back = norm_back(g, gain[...], unit, inverse)
    dsum[...] = back
    dlow[...] = back.astype(bf16)
    sums[...] = jnp.zeros_like(sums)
    sums[0:1] = jnp.sum(g * unit, axis=0, keepdims=True)
    sums[1:2] = jnp.sum(g, axis=0, keepdims=True)


def hidden_back_kernel(dlow, slope, w0, w1, w2, w3, du, sums, held, sems):
    fetch_all((w0, w1, w2, w3), held, sems)
    sums[...] = jnp.zeros_like(sums)

    def body(i, _):
        await_one((w0, w1, w2, w3), held, sems, i)
        for chunk in range(3):
            at = slice(chunk * 256, chunk * 256 + 256)
            back = dot(dlow[...], held[i, at, :], NT) * slope[i, :, at].astype(f32)
            back = back.astype(bf16)
            du[i, :, at] = back
            sums[i, 0:1, at] = jnp.sum(back.astype(f32), axis=0, keepdims=True)
        return 0

    lax.fori_loop(0, 4, body, 0)


def residual_back_kernel(du, dsum, pre, gain, w0, w1, w2, w3, dres, dlow, sums, held, sems, acc):
    fetch_all((w0, w1, w2, w3), held, sems)
    acc[...] = dsum[...]

    def body(i, _):
        await_one((w0, w1, w2, w3), held, sems, i)
        acc[...] += dot(du[i], held[i], NT)
        return 0

    lax.fori_loop(0, 4, body, 0)
    unit, inverse = moments(pre[...])
    g = acc[...]
    back = norm_back(g, gain[...], unit, inverse)
    dres[...] = back
    dlow[...] = back.astype(bf16)
    sums[...] = jnp.zeros_like(sums)
    sums[0:1] = jnp.sum(g * unit, axis=0, keepdims=True)
    sums[1:2] = jnp.sum(g, axis=0, keepdims=True)


def weight_grad_kernel(rows, left_a, left_b, right_a, right_b, out):
    left_a, left_b = left_a[...].reshape(left_a.shape[-2:]), left_b[...].reshape(left_b.shape[-2:])
    right_a, right_b = right_a[...].reshape(right_a.shape[-2:]), right_b[...].reshape(right_b.shape[-2:])
    total = dot(left_a, right_a, TN) + dot(left_b, right_b, TN)
    out[0] = total[0:rows].astype(bf16)


def weight_grad(left_a, left_b, right_a, right_b, chunk, rows, name):
    count = left_a.shape[-2]
    many = left_a.ndim == 3
    width = left_a.shape[-1]
    right_width = right_a.shape[-1]
    steps = width // chunk
    if many:
        left_spec = pl.BlockSpec((1, count, chunk), lambda j, c: (j, 0, c))
        right_spec = pl.BlockSpec((count, right_width), lambda j, c: (0, 0))
    else:
        left_spec = pl.BlockSpec((count, chunk), lambda j, c: (0, c))
        right_spec = pl.BlockSpec((1, count, right_width), lambda j, c: (j, 0, 0))
    return pl.pallas_call(
        functools.partial(weight_grad_kernel, rows),
        grid=(2, steps),
        out_shape=jax.ShapeDtypeStruct((2, steps * rows, right_width), bf16),
        in_specs=[left_spec, left_spec, right_spec, right_spec],
        out_specs=pl.BlockSpec((1, rows, right_width), lambda j, c: (j, c, 0)),
        compiler_params=pltpu.CompilerParams(vmem_limit_bytes=40 << 20),
        cost_estimate=pl.CostEstimate(
            flops=2 * 2 * 2 * count * width * right_width, bytes_accessed=12 << 20, transcendentals=0
        ),
        name=name,
    )(left_a, left_b, right_a, right_b)


HOP = {1: 2, 2: 1, 3: 3}


def hop(x, step):
    return lax.ppermute(x, "head", [(i, i ^ HOP[step]) for i in range(4)])


def gather(x):
    across = hop(x, 1)
    return [x, across, hop(x, 2), hop(across, 2)]


def batch_total(x, count):
    step = 1
    while step < count:
        x = x + lax.ppermute(x, "batch", [(i, i ^ step) for i in range(count)])
        step *= 2
    return x


def batch_total_large(x, count):
    rows = x.shape[0]
    pieces = lax.all_to_all(x, "batch", split_axis=0, concat_axis=0, tiled=True)
    piece = jnp.sum(pieces.reshape(count, rows // count, x.shape[1]).astype(f32), axis=0).astype(bf16)
    return lax.all_gather(piece, "batch", axis=0, tiled=True)


def neighbours(x):
    before = lax.ppermute(x[-HALO:], "head", [(i, i + 1) for i in range(3)])
    after = lax.ppermute(x[:HALO], "head", [(i + 1, i) for i in range(3)])
    return before, after


def local(
    batch_count,
    tokens,
    lengths,
    w_query,
    w_key,
    w_value,
    w_out,
    conv_taps,
    w_up,
    b_up,
    w_down,
    gain_attn,
    shift_attn,
    gain_ffn,
    shift_ffn,
    grad_out,
):
    tokens = tokens[0]
    grad_out = grad_out[0]
    count, width = tokens.shape
    ext = count + 128
    length = lengths[0]
    info = jnp.stack([length, lax.axis_index("head") * count]).astype(jnp.int32)
    gain_attn, shift_attn, gain_ffn, shift_ffn = (
        x.reshape(1, width) for x in (gain_attn, shift_attn, gain_ffn, shift_ffn)
    )

    marks = jnp.arange(LANDMARKS + 1, dtype=jnp.int32) * length // LANDMARKS
    positions = info[1] + jnp.arange(count, dtype=jnp.int32)
    member = (positions[None, :] >= marks[:-1, None]) & (positions[None, :] < marks[1:, None])
    pooled = jnp.dot(member.astype(bf16), tokens, preferred_element_type=f32)
    pooled = pooled / (marks[1:] - marks[:-1]).astype(f32)[:, None]
    pools = [pooled, hop(pooled, 1), hop(pooled, 2), hop(pooled, 3)]

    wt_own = jnp.concatenate([w_query.T, w_key.T, w_value.T], axis=0)
    taps = jnp.pad(conv_taps, ((0, 0), (0, width - TAPS)))
    taps_back = jnp.pad(conv_taps[:, ::-1], ((0, 0), (0, width - TAPS)))
    small_own = jnp.concatenate([b_up[None], taps, taps_back, jnp.zeros((1, width), f32)], axis=0)
    before, after = neighbours(tokens)
    wt = gather(wt_own)
    small = jnp.stack(gather(small_own))
    wo = gather(w_out)
    wu = gather(w_up)
    wd = gather(w_down)
    tokens_other = hop(tokens, 2)

    vm, an = VMEM, ANY
    lm_own, chain = call(
        landmark_kernel,
        [((64, 3 * GROUP), f32), ((NEWTON, 4, 3, 64, 64), f32)],
        [(vm, p) for p in pools] + [(vm, wt_own)],
        flops=int(1e9),
        size=4 << 20,
        name="landmarks",
    )
    lm = jnp.stack(gather(lm_own))
    q, k, v = call(
        project_kernel,
        [((4, count, GROUP), bf16), ((4, count, GROUP), bf16), ((4, ext, GROUP), bf16)],
        [(vm, info), (vm, tokens), (vm, before), (vm, after)] + [(an, w) for w in wt],
        [pltpu.VMEM((4, 3 * GROUP, width), bf16), pltpu.SemaphoreType.DMA((4, 3))],
        flops=2 * count * width * 3072,
        size=8 << 20,
        smem=(0,),
        name="project",
    )
    (pay,) = call(
        third_kernel,
        [((4, 64, GROUP), f32)],
        [(vm, info), (vm, lm), (vm, k), (vm, v)],
        flops=int(1e9),
        size=3 << 20,
        smem=(0,),
        name="third",
    )
    pays = [pay, hop(pay, 1), hop(pay, 2), hop(pay, 3)]
    ctx, wst, x_mid = call(
        context_kernel,
        [((4, count, GROUP), bf16), ((4, 64, GROUP), f32), ((4, 64, GROUP), f32)],
        [(vm, p) for p in pays] + [(vm, lm), (vm, q), (vm, v), (vm, small)],
        flops=int(3e9),
        size=5 << 20,
        name="context",
    )
    out_scratch = [pltpu.VMEM((4, GROUP, width), bf16), pltpu.SemaphoreType.DMA((4,))]
    wide = [pltpu.VMEM((4, width, width), bf16), pltpu.SemaphoreType.DMA((4,))]
    acc = [pltpu.VMEM((count, width), f32)]
    pre, normed, normed_low = call(
        attended_kernel,
        [((count, width), f32), ((count, width), f32), ((count, width), bf16)],
        [(vm, ctx), (vm, tokens), (vm, gain_attn), (vm, shift_attn)] + [(an, w) for w in wo],
        out_scratch,
        flops=2 * count * width * width,
        size=6 << 20,
        name="attended",
    )
    normed_other = hop(normed_low, 2)
    hidden, slope = call(
        up_kernel,
        [((4, count, width), bf16), ((4, count, width), bf16)],
        [(vm, normed_low), (vm, small)] + [(an, w) for w in wu],
        wide,
        flops=2 * count * width * 3072,
        size=12 << 20,
        name="up",
    )
    hidden_keep, hidden_send = hidden[0:2], hidden[2:4]
    hidden_other = hop(hidden_send, 2)
    output, d_sum, gd, sums_ffn = call(
        down_kernel,
        [((count, width), bf16), ((count, width), f32), ((count, width), bf16), ((8, width), f32)],
        [(vm, hidden), (vm, normed), (vm, grad_out), (vm, gain_ffn), (vm, shift_ffn)] + [(an, w) for w in wd],
        wide + acc,
        flops=2 * count * width * 3072,
        size=14 << 20,
        name="down",
    )
    gd_other = hop(gd, 2)
    du, sums_up = call(
        hidden_back_kernel,
        [((4, count, width), bf16), ((4, 8, width), f32)],
        [(vm, gd), (vm, slope)] + [(an, w) for w in wd],
        wide,
        flops=2 * count * width * 3072,
        size=12 << 20,
        name="hidden_back",
    )
    du_other = hop(du[2:4], 2)
    g_down = weight_grad(hidden_keep, hidden_other, gd, gd_other, 256, 256, "grad_down")
    d_res, ga, sums_attn = call(
        residual_back_kernel,
        [((count, width), f32), ((count, width), bf16), ((8, width), f32)],
        [(vm, du), (vm, d_sum), (vm, pre), (vm, gain_attn)] + [(an, w) for w in wu],
        wide + acc,
        flops=2 * count * width * 3072,
        size=14 << 20,
        name="residual_back",
    )
    ga_other = hop(ga, 2)
    ga_before, ga_after = neighbours(ga)
    g_up = weight_grad(normed_low, normed_other, du[0:2], du_other, 256, 256, "grad_up")
    dx, dq, dkl, dv_conv, dtaps = call(
        first_back_kernel,
        [
            ((4, 64, GROUP), f32),
            ((4, count, GROUP), f32),
            ((4, 64, GROUP), f32),
            ((4, count, GROUP), f32),
            ((4, 8, GROUP), f32),
        ],
        [(vm, ga), (vm, ga_before), (vm, ga_after)]
        + [(an, w) for w in wo]
        + [(vm, lm), (vm, q), (vm, v), (vm, small), (vm, x_mid)],
        out_scratch + [pltpu.VMEM((ext, width), bf16), pltpu.VMEM((ext, GROUP), f32)],
        flops=int(5e9),
        size=10 << 20,
        name="first_back",
    )
    dxs = [dx, hop(dx, 1), hop(dx, 2), hop(dx, 3)]
    g_out = weight_grad(ctx[0:2], hop(ctx[2:4], 2), ga, ga_other, GROUP, 192, "grad_out")
    dk, dql, dv = call(
        third_back_kernel,
        [((4, count, GROUP), f32), ((4, 64, GROUP), f32), ((4, count, GROUP), bf16)],
        [(vm, info)] + [(vm, d) for d in dxs] + [(vm, lm), (vm, wst), (vm, k), (vm, v), (vm, dv_conv)],
        flops=int(5e9),
        size=8 << 20,
        smem=(0,),
        name="third_back",
    )
    (own_back,) = call(
        inverse_back_kernel,
        [((64, 2 * GROUP), f32)],
        [(vm, d[i]) for i, d in enumerate(dxs)] + [(vm, wst[0]), (vm, lm_own), (vm, chain)],
        flops=int(1e9),
        size=4 << 20,
        name="inverse_back",
    )
    landmark_back = jnp.concatenate([dql, dkl], axis=2)
    landmark_back = landmark_back.at[0].add(own_back)
    other = hop(landmark_back, 2)
    paired = (landmark_back + jnp.concatenate([other[2:4], other[0:2]], axis=0)).astype(bf16)
    across = hop(paired, 1)
    (joint,) = call(
        joint_back_kernel,
        [((4, count, 3 * GROUP), bf16)],
        [(vm, info), (vm, paired), (vm, across), (vm, dq), (vm, dk), (vm, dv)],
        flops=int(1e9),
        size=8 << 20,
        smem=(0,),
        name="joint_back",
    )
    joint_other = hop(joint[2:4], 2)
    (d_tokens,) = call(
        token_back_kernel,
        [((count, width), f32)],
        [(vm, joint), (vm, d_res)] + [(an, w) for w in wt],
        [pltpu.VMEM((4, 3 * GROUP, width), bf16), pltpu.SemaphoreType.DMA((4, 3))],
        flops=2 * count * width * 3072,
        size=10 << 20,
        name="token_back",
    )
    g_joint = weight_grad(joint[0:2], joint_other, tokens, tokens_other, GROUP, 192, "grad_joint")

    def reduce_grad(g):
        own = (g[0].astype(f32) + hop(g[1], 1).astype(f32)).astype(bf16)
        return batch_total_large(own, batch_count)

    d_w_down = reduce_grad(g_down).astype(f32)
    d_w_up = reduce_grad(g_up).astype(f32)
    d_w_out = reduce_grad(g_out).astype(f32)
    d_joint = reduce_grad(g_joint).astype(f32)
    heads = width // 4
    d_w_query, d_w_key, d_w_value = (d_joint[i * heads : (i + 1) * heads].T for i in range(3))

    norms = jnp.concatenate([sums_attn[0:2], sums_ffn[0:2]], axis=0)
    dtaps = jnp.pad(dtaps[:, 1:4], ((0, 0), (0, 0), (0, width - GROUP)))
    minor = jnp.concatenate([sums_up[:, 0:1], dtaps, jnp.broadcast_to(norms, (4, 4, width))], axis=1)
    minor = minor[0] + hop(minor[1], 1) + hop(minor[2], 2) + hop(minor[3], 3)
    minor = batch_total(minor, batch_count)
    return (
        output[None],
        d_tokens[None],
        d_w_query,
        d_w_key,
        d_w_value,
        d_w_out,
        minor[1:4, 0:TAPS],
        d_w_up,
        minor[0],
        d_w_down,
        minor[4],
        minor[5],
        minor[6],
        minor[7],
    )


def solution(mesh):
    return jax.shard_map(
        functools.partial(local, mesh.shape["batch"]),
        mesh=mesh,
        in_specs=(
            P("batch", "head", None),
            P("batch"),
            P(None, "head"),
            P(None, "head"),
            P(None, "head"),
            P("head", None),
            P("head", None),
            P(None, "head"),
            P("head"),
            P("head", None),
            P(),
            P(),
            P(),
            P(),
            P("batch", "head", None),
        ),
        out_specs=(
            P("batch", "head", None),
            P("batch", "head", None),
            P(None, "head"),
            P(None, "head"),
            P(None, "head"),
            P("head", None),
            P("head", None),
            P(None, "head"),
            P("head"),
            P("head", None),
            P(),
            P(),
            P(),
            P(),
        ),
        check_vma=False,
    )
```

time: 806 us -> 496 us (0.62)
  waiting for transfers between devices: 371 us -> 138 us
  matrix products: 155 us -> 1.43 us
  other arithmetic: 138 us -> 21.9 us
  Pallas kernels: 0 us -> 111 us
  starting transfers between devices: 0.99 us -> 102 us
  blocking collectives: 80.9 us -> 63.6 us
    psum x1 -> x0, waiting for transfers between devices: 151 us -> none  [local(): lax.psum((d_w_query, d_w_key, d_w_value, d_w_out, d_conv_taps, d_w_up, d_...]
    dot_general x104 -> x1, matrix products: 152 us -> 1.43 us  [local(): pooled = jnp.dot(member.astype(bf16), tokens, preferred_element_type=f32)]
    ppermute x0 -> x51, waiting for transfers between devices: none -> 133 us  [the longest x44 116 us: hop(): return lax.ppermute(x, 'head', [(i, i ^ HOP[step]) for i in range(4)])]
    reduce_scatter x4 -> x0, waiting for transfers between devices: 114 us -> none  [the longest x1 38.1 us: local(): lax.psum_scatter(jnp.einsum('tf,df->td', d_upward, w_up, preferred_elemen...]
    pallas_call x0 -> x18, Pallas kernels: none -> 111 us  [the longest x14 91.7 us: call(): pl.pallas_call(body, out_shape=[jax.ShapeDtypeStruct(s, d) for s, d in ou...]
    all_gather x4 -> x2, waiting for transfers between devices: 105 us -> 0.01 us  [batch_total_large(): return lax.all_gather(piece, 'batch', axis=0, tiled=True)]
    ppermute x0 -> x51, starting transfers between devices: none -> 81.6 us  [the longest x44 67.1 us: hop(): return lax.ppermute(x, 'head', [(i, i ^ HOP[step]) for i in range(4)])]
    psum x2 -> x0, blocking collectives: 80.9 us -> none  [the longest x1 40.6 us: local(): lax.psum((d_w_query, d_w_key, d_w_value, d_w_out, d_conv_taps, d_w_up, d_...]
  transfers between devices with their start and end apart: 9 -> 57, of which waited for: 8 -> 20; matrix products, arithmetic and copies ran while one was open for 8% -> 6% of each run, Pallas kernels for 0% -> 22%
where the time goes in v1:
time: 496 us; the launch traced here: 494 us
  waiting for transfers between devices  138 us (28%)
  Pallas kernels  111 us (22%)
  starting transfers between devices  102 us (21%)
  blocking collectives  63.6 us (13%)
  local copies, waits for them, and re-layouts  40.2 us (8%)
  other arithmetic  21.9 us (4%)
  between operations  15.7 us (3%)
    ppermute x44, waiting for transfers between devices, hop(): return lax.ppermute(x, 'head', [(i, i ^ HOP[step]) for i in range(4)])  116 us
    pallas_call x14, Pallas kernels, call(): pl.pallas_call(body, out_shape=[jax.ShapeDtypeStruct(s, d) for s, d in ou...  91.7 us
    ppermute x44, starting transfers between devices, hop(): return lax.ppermute(x, 'head', [(i, i ^ HOP[step]) for i in range(4)])  67.1 us
    all_gather x2, blocking collectives, batch_total_large(): return lax.all_gather(piece, 'batch', axis=0, tiled=True)  63.6 us
    unnamed x131, local copies, waits for them, and re-layouts  28 us
    all_to_all x4, starting transfers between devices, batch_total_large(): pieces = lax.all_to_all(x, 'batch', split_axis=0, concat_axis=0, tiled=True)  20 us
    pallas_call x4, Pallas kernels, weight_grad(): pl.pallas_call(functools.partial(weight_grad_kernel, rows), grid=(2, step...  19.2 us
    ppermute x3, waiting for transfers between devices, batch_total(): x = x + lax.ppermute(x, 'batch', [(i, i ^ step) for i in range(count)])  14.6 us
  transfers between devices with their start and end apart: 57, of which 20 were waited for; matrix products, arithmetic and copies ran while one was open for 6% of the time, Pallas kernels for 22%

profile of v1, /device:TPU:0, one launch (start us, length us, event | category | flops | bytes accessed | tf_op | source)
XLA Modules:
  0.0 494.0 jit_solution(10438930619769395072)
XLA Ops:
  16.2 20.0 %collective-permute-done.p1 = f32[64,768]{1,0:T(8,128)S(1)} collective-permute-done((f32[64,768]{1,0:T(8,128)S(1)}, f32[64,768]{1,0:T(8,128)S(1)}, u32[]{:S(2)}, u32[]{:S(2)}) %collective-permute-start) | collective-permute-done | bytes 196640 | tf_op jit(solution)/shard_map/ppermute | solution.py:586
  41.0 9.7 %landmarks.1 = (f32[64,768]{1,0:T(8,128)S(1)}, f32[6,4,3,64,64]{4,3,2,1,0:T(8,128)S(1)}) custom-call(f32[64,768]{1,0:T(8,128)S(1)} %convolution_divide_fusion.p0, f32[64,768]{1,0:T(8,128)S(1)} %copy-done.43, f32[64,768]{1,0:T(8,128)} %collective-permute-done.1.p2, f32[64,768]{1,0:T(8,128)} %collective-permute-done.2.p3, ...), custom_call_target="tpu_custom_call" | custom-call | flops 1000000000 | bytes 4194304 | tf_op jit(solution)/shard_map/landmarks/pallas_call | solution.py:54
  57.9 13.3 %collective-permute-start.23 = (bf16[768,768]{1,0:T(8,128)(2,1)}, bf16[768,768]{1,0:T(8,128)(2,1)}, u32[]{:S(2)}, u32[]{:S(2)}) collective-permute-start(bf16[768,768]{1,0:T(8,128)(2,1)} %w0.6), channel_id=1, source_target_pairs={{0,2},{1,3},{2,0},{3,1},{4,6},{5,7},{6,4},{7,5},{8,10},{9,11},{10,... | collective-permute-start | bytes 3538952 | tf_op jit(solution)/shard_map/ppermute | solution.py:586
  77.2 20.1 %collective-permute-start.15 = (f32[8,768]{1,0:T(8,128)S(1)}, f32[8,768]{1,0:T(8,128)S(1)}, u32[]{:S(2)}, u32[]{:S(2)}) collective-permute-start(f32[8,768]{1,0:T(8,128)S(1)} %get-tuple-element.112), channel_id=1, source_target_pairs={{0,1},{1,0},{2,3},{3,2},{4,5},{5,4},{6,7},{7,6},{8,9},{9,8},{10,11... | collective-permute-start | bytes 73736 | tf_op jit(solution)/shard_map/ppermute | solution.py:586
  97.4 6.2 %project.1 = (bf16[4,512,256]{2,1,0:T(8,128)(2,1)S(1)}, bf16[4,512,256]{2,1,0:T(8,128)(2,1)S(1)}, bf16[4,640,256]{2,1,0:T(8,128)(2,1)S(1)}) custom-call(s32[2]{0:T(128)S(1)} %pad_add_fusion.info, bf16[512,768]{1,0:T(8,128)(2,1)} %bitcast.2.tokens.right_a, bf16[32,768]{1,0:T(8,128)(2,1)S(1)} %collective-permute-done.6.before, ...), custom_call_target="tpu_custom_call" | custom-call | flops 2415919104 | bytes 8388608 | tf_op jit(solution)/shard_map/project/pallas_call | solution.py:54
  110.8 6.4 %collective-permute-done.11.p1 = f32[4,64,256]{2,1,0:T(8,128)S(1)} collective-permute-done((f32[4,64,256]{2,1,0:T(8,128)S(1)}, f32[4,64,256]{2,1,0:T(8,128)S(1)}, u32[]{:S(2)}, u32[]{:S(2)}) %collective-permute-start.11) | collective-permute-done | bytes 262176 | tf_op jit(solution)/shard_map/ppermute | solution.py:586
  122.4 6.7 %context.1 = (bf16[4,512,256]{2,1,0:T(8,128)(2,1)S(1)}, f32[4,64,256]{2,1,0:T(8,128)S(1)}, f32[4,64,256]{2,1,0:T(8,128)S(1)}) custom-call(f32[4,64,256]{2,1,0:T(8,128)S(1)} %third.1.p0, f32[4,64,256]{2,1,0:T(8,128)S(1)} %collective-permute-done.11.p1, f32[4,64,256]{2,1,0:T(8,128)S(1)} %collective-permute-done.12.p2, ...), custom_call_target="tpu_custom_call" | custom-call | flops 3000000000 | bytes 5242880 | tf_op jit(solution)/shard_map/context/pallas_call | solution.py:54
  137.3 6.8 %up.1 = (bf16[4,512,768]{2,1,0:T(8,128)(2,1)S(1)}, bf16[4,512,768]{2,1,0:T(8,128)(2,1)S(1)}) custom-call(bf16[512,768]{1,0:T(8,128)(2,1)} %get-tuple-element.61.low.left_a, f32[4,8,768]{2,1,0:T(8,128)S(1)} %pad_maximum_fusion.2.small, bf16[768,768]{1,0:T(8,128)(2,1)S(1)} %copy-done.10, bf16[768,768]{1,0:T(8,128)(2,1)S(1)} %collective-permute-done.20.w1, ...), custom_call_target="tpu_custom_call" | custom-call | flops 2415919104 | bytes 12582912 | tf_op jit(solution)/shard_map/up/pallas_call | solution.py:54
  145.8 6.6 %down.1 = (bf16[512,768]{1,0:T(8,128)(2,1)}, f32[512,768]{1,0:T(8,128)S(1)}, bf16[512,768]{1,0:T(8,128)(2,1)}, f32[8,768]{1,0:T(8,128)S(1)}) custom-call(bf16[4,512,768]{2,1,0:T(8,128)(2,1)S(1)} %get-tuple-element.62.hidden, f32[512,768]{1,0:T(8,128)S(1)} %get-tuple-element.63.normed, bf16[512,768]{1,0:T(8,128)(2,1)S(1)} %bitcast.90, ...), custom_call_target="tpu_custom_call" | custom-call | flops 2415919104 | bytes 14680064 | tf_op jit(solution)/shard_map/down/pallas_call | solution.py:54
  154.3 6.0 %hidden_back.1 = (bf16[4,512,768]{2,1,0:T(8,128)(2,1)S(1)}, f32[4,8,768]{2,1,0:T(8,128)S(1)}) custom-call(bf16[512,768]{1,0:T(8,128)(2,1)} %get-tuple-element.65.dlow.right_a, bf16[4,512,768]{2,1,0:T(8,128)(2,1)S(1)} %copy-done.45, bf16[768,768]{1,0:T(8,128)(2,1)} %w0.6, bf16[768,768]{1,0:T(8,128)(2,1)} %collective-permute-done.23.w1, ...), custom_call_target="tpu_custom_call" | custom-call | flops 2415919104 | bytes 12582912 | tf_op jit(solution)/shard_map/hidden_back/pallas_call | solution.py:54
  176.7 12.5 %first_back.1 = (f32[4,64,256]{2,1,0:T(8,128)S(1)}, f32[4,512,256]{2,1,0:T(8,128)S(1)}, f32[4,64,256]{2,1,0:T(8,128)S(1)}, f32[4,512,256]{2,1,0:T(8,128)S(1)}, f32[4,8,256]{2,1,0:T(8,128)S(1)}) custom-call(bf16[512,768]{1,0:T(8,128)(2,1)S(1)} %get-tuple-element.70.g_ref.right_a, bf16[32,768]{1,0:T(8,128)(2,1)S(1)} %collective-permute-done.26.before, ...), custom_call_target="tpu_custom_call" | custom-call | flops 5000000000 | bytes 10485760 | tf_op jit(solution)/shard_map/first_back/pallas_call | solution.py:54
  206.0 9.4 %inverse_back.1 = f32[64,512]{1,0:T(8,128)S(1)} custom-call(f32[64,256]{1,0:T(8,128)S(1)} %slice_bitcast_fusion.15.x0, f32[64,256]{1,0:T(8,128)S(1)} %slice_bitcast_fusion.13.x1, f32[64,256]{1,0:T(8,128)S(1)} %slice_bitcast_fusion.12.x2, f32[64,256]{1,0:T(8,128)S(1)} %slice_bitcast_fusion.11.x3, f32[64,256]{1,0:T(8,128)S(1)} %slice_bitcast_fusion.14.wst, ...), custom_call_target="tpu_custom_call" | custom-call | flops 1000000000 | bytes 4194304 | tf_op jit(solution)/shard_map/inverse_back/pallas_call | solution.py:54
  217.0 6.7 %third_back.1 = (f32[4,512,256]{2,1,0:T(8,128)S(1)}, f32[4,64,256]{2,1,0:T(8,128)S(1)}, bf16[4,512,256]{2,1,0:T(8,128)(2,1)S(1)}) custom-call(s32[2]{0:T(128)S(1)} %pad_add_fusion.info, f32[4,64,256]{2,1,0:T(8,128)S(1)} %get-tuple-element.72.x0, f32[4,64,256]{2,1,0:T(8,128)S(1)} %collective-permute-done.28.x1, f32[4,64,256]{2,1,0:T(8,128)S(1)} %collective-permute-done.29.x2, ...), custom_call_target="tpu_custom_call" | custom-call | flops 5000000000 | bytes 8388608 | tf_op jit(solution)/shard_map/third_back/pallas_call | solution.py:54
  224.3 6.1 %grad_up.1 = bf16[2,768,768]{2,1,0:T(8,128)(2,1)S(1)} custom-call(bf16[512,768]{1,0:T(8,128)(2,1)} %get-tuple-element.61.low.left_a, bf16[512,768]{1,0:T(8,128)(2,1)} %collective-permute-done.45.left_b, bf16[2,512,768]{2,1,0:T(8,128)(2,1)S(1)} %get-tuple-element.94.right_a, bf16[2,512,768]{2,1,0:T(8,128)(2,1)S(1)} %collective-permute-done.46.right_b), custom_call_target="tpu_custom_call" | custom-call | flops 2415919104 | bytes 12582912 | tf_op jit(solution)/shard_map/grad_up/pallas_call | solution.py:568
  238.5 28.4 %collective-permute-done.38 = bf16[192,768]{1,0:T(8,128)(2,1)S(1)} collective-permute-done((bf16[192,768]{1,0:T(8,128)(2,1)S(1)}, bf16[192,768]{1,0:T(8,128)(2,1)S(1)}, u32[]{:S(2)}, u32[]{:S(2)}) %collective-permute-start.38) | collective-permute-done | bytes 294944 | tf_op jit(solution)/shard_map/ppermute | solution.py:586
  267.7 5.8 %all-to-all-start.1 = ((bf16[8,24,768]{2,1,0:T(8,128)(2,1)}), bf16[8,24,768]{2,1,0:T(8,128)(2,1)}, u32[]{:S(2)}, u32[]{:S(2)}) async-start(bf16[8,24,768]{2,1,0:T(8,128)(2,1)} %bitcast.33), calls=%async_computation.1 | async-start | bytes 589824 | tf_op jit(solution)/shard_map/all_to_all | solution.py:604
  295.5 6.0 %grad_down.1 = bf16[2,768,768]{2,1,0:T(8,128)(2,1)S(1)} custom-call(bf16[2,512,768]{2,1,0:T(8,128)(2,1)S(1)} %copy-done.8, bf16[2,512,768]{2,1,0:T(8,128)(2,1)} %collective-permute-done.48.left_b, bf16[512,768]{1,0:T(8,128)(2,1)} %get-tuple-element.65.dlow.right_a, bf16[512,768]{1,0:T(8,128)(2,1)} %collective-permute-done.49.right_b), custom_call_target="tpu_custom_call" | custom-call | flops 2415919104 | bytes 12582912 | tf_op jit(solution)/shard_map/grad_down/pallas_call | solution.py:568
  305.4 22.6 %collective-permute-done.50 = bf16[768,768]{1,0:T(8,128)(2,1)S(1)} collective-permute-done((bf16[768,768]{1,0:T(8,128)(2,1)S(1)}, bf16[768,768]{1,0:T(8,128)(2,1)S(1)}, u32[]{:S(2)}, u32[]{:S(2)}) %collective-permute-start.50) | collective-permute-done | bytes 1179680 | tf_op jit(solution)/shard_map/ppermute | solution.py:586
  329.4 5.7 %all-to-all-start.3 = ((bf16[8,96,768]{2,1,0:T(8,128)(2,1)}), bf16[8,96,768]{2,1,0:T(8,128)(2,1)}, u32[]{:S(2)}, u32[]{:S(2)}) async-start(bf16[8,96,768]{2,1,0:T(8,128)(2,1)} %bitcast.93), calls=%async_computation.3 | async-start | bytes 2359296 | tf_op jit(solution)/shard_map/all_to_all | solution.py:604
  339.0 5.9 %grad_joint.1 = bf16[2,576,768]{2,1,0:T(8,128)(2,1)S(1)} custom-call(bf16[2,512,768]{2,1,0:T(8,128)(2,1)S(1)} %copy-done.9, bf16[2,512,768]{2,1,0:T(8,128)(2,1)} %collective-permute-done.33.left_b, bf16[512,768]{1,0:T(8,128)(2,1)} %bitcast.2.tokens.right_a, bf16[512,768]{1,0:T(8,128)(2,1)} %collective-permute-done.34.right_b), custom_call_target="tpu_custom_call" | custom-call | flops 2415919104 | bytes 12582912 | tf_op jit(solution)/shard_map/grad_joint/pallas_call | solution.py:568
  346.5 17.2 %collective-permute-done.35 = bf16[576,768]{1,0:T(8,128)(2,1)S(1)} collective-permute-done((bf16[576,768]{1,0:T(8,128)(2,1)S(1)}, bf16[576,768]{1,0:T(8,128)(2,1)S(1)}, u32[]{:S(2)}, u32[]{:S(2)}) %collective-permute-start.35) | collective-permute-done | bytes 884768 | tf_op jit(solution)/shard_map/ppermute | solution.py:586
  385.8 7.9 %collective-permute-done.43 = f32[8,768]{1,0:T(8,128)S(1)} collective-permute-done((f32[8,768]{1,0:T(8,128)S(1)}, f32[8,768]{1,0:T(8,128)S(1)}, u32[]{:S(2)}, u32[]{:S(2)}) %collective-permute-start.43) | collective-permute-done | bytes 24608 | tf_op jit(solution)/shard_map/ppermute | solution.py:597
  414.4 31.1 %all_gather.13 = bf16[192,768]{1,0:T(8,128)(2,1)S(1)} all-gather(bf16[24,768]{1,0:T(8,128)(2,1)S(1)} %reduce_sum.49), channel_id=1, replica_groups=mesh['batch'=8,'head'=4] {'batch'}, dimensions={0}, use_global_device_ids=true | all-gather | bytes 331776 | tf_op jit(solution)/shard_map/all_gather | solution.py:606
  447.7 32.5 %all_gather.12 = bf16[576,768]{1,0:T(8,128)(2,1)S(1)} all-gather(bf16[72,768]{1,0:T(8,128)(2,1)S(1)} %reduce_sum.48), channel_id=1, replica_groups=mesh['batch'=8,'head'=4] {'batch'}, dimensions={0}, use_global_device_ids=true | all-gather | bytes 995328 | tf_op jit(solution)/shard_map/all_gather | solution.py:606
  (305 shorter events, 178.7 us)
Async XLA Ops:
  8.5 44.5 %collective-permute-start.8 = (bf16[576,768]{1,0:T(8,128)(2,1)S(1)}, bf16[576,768]{1,0:T(8,128)(2,1)S(1)}, u32[]{:S(2)}, u32[]{:S(2)}) collective-permute-start(bf16[576,768]{1,0:T(8,128)(2,1)S(1)} %pad_maximum_fusion.wt.w0), channel_id=1, source_target_pairs={{0,2},{1,3},{2,0},{3,1},{4,6},{5,7},{6,4},{7,5},{8,10},{9,11},{10,... | collective-permute-start | bytes 2654216 | tf_op jit(solution)/shard_map/ppermute | solution.py:586
  15.9 81.3 %collective-permute-start.9 = (bf16[576,768]{1,0:T(8,128)(2,1)S(1)}, bf16[576,768]{1,0:T(8,128)(2,1)}, u32[]{:S(2)}, u32[]{:S(2)}) collective-permute-start(bf16[576,768]{1,0:T(8,128)(2,1)S(1)} %pad_maximum_fusion.wt.w0), channel_id=1, source_target_pairs={{0,1},{1,0},{2,3},{3,2},{4,5},{5,4},{6,7},{7,6},{8,9},{9,8},{10,11... | collective-permute-start | bytes 2654216 | tf_op jit(solution)/shard_map/ppermute | solution.py:586
  39.0 71.6 %collective-permute-start.20 = (bf16[768,768]{1,0:T(8,128)(2,1)S(1)}, bf16[768,768]{1,0:T(8,128)(2,1)S(1)}, u32[]{:S(2)}, u32[]{:S(2)}) collective-permute-start(bf16[768,768]{1,0:T(8,128)(2,1)S(1)} %copy-done.10), channel_id=1, source_target_pairs={{0,2},{1,3},{2,0},{3,1},{4,6},{5,7},{6,4},{7,5},{8,10},{9,11},{10,... | collective-permute-start | bytes 3538952 | tf_op jit(solution)/shard_map/ppermute | solution.py:586
  53.1 44.2 %collective-permute-start.10 = (bf16[576,768]{1,0:T(8,128)(2,1)S(1)}, bf16[576,768]{1,0:T(8,128)(2,1)S(1)}, u32[]{:S(2)}, u32[]{:S(2)}) collective-permute-start(bf16[576,768]{1,0:T(8,128)(2,1)S(1)} %collective-permute-done.8.w1), channel_id=1, source_target_pairs={{0,1},{1,0},{2,3},{3,2},{4,5},{5,4},{6,7},{7,6},{8,9},{9,8},{10,11... | collective-permute-start | bytes 2654216 | tf_op jit(solution)/shard_map/ppermute | solution.py:586
  57.9 52.8 %collective-permute-start.23 = (bf16[768,768]{1,0:T(8,128)(2,1)}, bf16[768,768]{1,0:T(8,128)(2,1)}, u32[]{:S(2)}, u32[]{:S(2)}) collective-permute-start(bf16[768,768]{1,0:T(8,128)(2,1)} %w0.6), channel_id=1, source_target_pairs={{0,2},{1,3},{2,0},{3,1},{4,6},{5,7},{6,4},{7,5},{8,10},{9,11},{10,... | collective-permute-start | bytes 3538952 | tf_op jit(solution)/shard_map/ppermute | solution.py:586
  77.2 26.5 %collective-permute-start.15 = (f32[8,768]{1,0:T(8,128)S(1)}, f32[8,768]{1,0:T(8,128)S(1)}, u32[]{:S(2)}, u32[]{:S(2)}) collective-permute-start(f32[8,768]{1,0:T(8,128)S(1)} %get-tuple-element.112), channel_id=1, source_target_pairs={{0,1},{1,0},{2,3},{3,2},{4,5},{5,4},{6,7},{7,6},{8,9},{9,8},{10,11... | collective-permute-start | bytes 73736 | tf_op jit(solution)/shard_map/ppermute | solution.py:586
  117.2 28.6 %collective-permute-start.24 = (bf16[768,768]{1,0:T(8,128)(2,1)}, bf16[768,768]{1,0:T(8,128)(2,1)}, u32[]{:S(2)}, u32[]{:S(2)}) collective-permute-start(bf16[768,768]{1,0:T(8,128)(2,1)} %w0.6), channel_id=1, source_target_pairs={{0,1},{1,0},{2,3},{3,2},{4,5},{5,4},{6,7},{7,6},{8,9},{9,8},{10,11... | collective-permute-start | bytes 3538952 | tf_op jit(solution)/shard_map/ppermute | solution.py:586
  117.3 28.6 %collective-permute-start.25 = (bf16[768,768]{1,0:T(8,128)(2,1)}, bf16[768,768]{1,0:T(8,128)(2,1)}, u32[]{:S(2)}, u32[]{:S(2)}) collective-permute-start(bf16[768,768]{1,0:T(8,128)(2,1)} %collective-permute-done.23.w1), channel_id=1, source_target_pairs={{0,1},{1,0},{2,3},{3,2},{4,5},{5,4},{6,7},{7,6},{8,9},{9,8},{10,11... | collective-permute-start | bytes 3538952 | tf_op jit(solution)/shard_map/ppermute | solution.py:586
  134.4 89.8 %collective-permute-start.45 = (bf16[512,768]{1,0:T(8,128)(2,1)}, bf16[512,768]{1,0:T(8,128)(2,1)}, u32[]{:S(2)}, u32[]{:S(2)}) collective-permute-start(bf16[512,768]{1,0:T(8,128)(2,1)} %get-tuple-element.61.low.left_a), channel_id=1, source_target_pairs={{0,1},{1,0},{2,3},{3,2},{4,5},{5,4},{6,7},{7,6},{8,9},{9,8},{10,11... | collective-permute-start | bytes 2359304 | tf_op jit(solution)/shard_map/ppermute | solution.py:586
  174.5 61.4 %collective-permute-start.36 = (bf16[2,512,256]{2,1,0:T(8,128)(2,1)S(1)}, bf16[2,512,256]{2,1,0:T(8,128)(2,1)S(1)}, u32[]{:S(2)}, u32[]{:S(2)}) collective-permute-start(bf16[2,512,256]{2,1,0:T(8,128)(2,1)S(1)} %get-tuple-element.100), channel_id=1, source_target_pairs={{0,1},{1,0},{2,3},{3,2},{4,5},{5,4},{6,7},{7,6},{8,9},{9,8},{10,11... | collective-permute-start | bytes 1572872 | tf_op jit(solution)/shard_map/ppermute | solution.py:586
  191.8 32.4 %collective-permute-start.46 = (bf16[2,512,768]{2,1,0:T(8,128)(2,1)S(1)}, bf16[2,512,768]{2,1,0:T(8,128)(2,1)S(1)}, u32[]{:S(2)}, u32[]{:S(2)}) collective-permute-start(bf16[2,512,768]{2,1,0:T(8,128)(2,1)S(1)} %get-tuple-element.93), channel_id=1, source_target_pairs={{0,1},{1,0},{2,3},{3,2},{4,5},{5,4},{6,7},{7,6},{8,9},{9,8},{10,11... | collective-permute-start | bytes 4718600 | tf_op jit(solution)/shard_map/ppermute | solution.py:586
  199.5 36.4 %collective-permute-start.37 = (bf16[512,768]{1,0:T(8,128)(2,1)S(1)}, bf16[512,768]{1,0:T(8,128)(2,1)S(1)}, u32[]{:S(2)}, u32[]{:S(2)}) collective-permute-start(bf16[512,768]{1,0:T(8,128)(2,1)S(1)} %get-tuple-element.70.g_ref.right_a), channel_id=1, source_target_pairs={{0,1},{1,0},{2,3},{3,2},{4,5},{5,4},{6,7},{7,6},{8,9},{9,8},{10,11... | collective-permute-start | bytes 2359304 | tf_op jit(solution)/shard_map/ppermute | solution.py:586
  231.6 44.8 %collective-permute-start.47 = (bf16[768,768]{1,0:T(8,128)(2,1)}, bf16[768,768]{1,0:T(8,128)(2,1)}, u32[]{:S(2)}, u32[]{:S(2)}) collective-permute-start(bf16[768,768]{1,0:T(8,128)(2,1)} %slice_bitcast_fusion.2), channel_id=1, source_target_pairs={{0,2},{1,3},{2,0},{3,1},{4,6},{5,7},{6,4},{7,5},{8,10},{9,11},{10,... | collective-permute-start | bytes 3538952 | tf_op jit(solution)/shard_map/ppermute | solution.py:586
  235.9 59.7 %collective-permute-start.48 = (bf16[2,512,768]{2,1,0:T(8,128)(2,1)}, bf16[2,512,768]{2,1,0:T(8,128)(2,1)}, u32[]{:S(2)}, u32[]{:S(2)}) collective-permute-start(bf16[2,512,768]{2,1,0:T(8,128)(2,1)} %get-tuple-element.91), channel_id=1, source_target_pairs={{0,1},{1,0},{2,3},{3,2},{4,5},{5,4},{6,7},{7,6},{8,9},{9,8},{10,11... | collective-permute-start | bytes 4718600 | tf_op jit(solution)/shard_map/ppermute | solution.py:586
  237.2 29.8 %collective-permute-start.38 = (bf16[192,768]{1,0:T(8,128)(2,1)S(1)}, bf16[192,768]{1,0:T(8,128)(2,1)S(1)}, u32[]{:S(2)}, u32[]{:S(2)}) collective-permute-start(bf16[192,768]{1,0:T(8,128)(2,1)S(1)} %slice_bitcast_fusion.9), channel_id=1, source_target_pairs={{0,2},{1,3},{2,0},{3,1},{4,6},{5,7},{6,4},{7,5},{8,10},{9,11},{10,... | collective-permute-start | bytes 884744 | tf_op jit(solution)/shard_map/ppermute | solution.py:586
  237.5 58.0 %collective-permute-start.49 = (bf16[512,768]{1,0:T(8,128)(2,1)}, bf16[512,768]{1,0:T(8,128)(2,1)}, u32[]{:S(2)}, u32[]{:S(2)}) collective-permute-start(bf16[512,768]{1,0:T(8,128)(2,1)} %get-tuple-element.65.dlow.right_a), channel_id=1, source_target_pairs={{0,1},{1,0},{2,3},{3,2},{4,5},{5,4},{6,7},{7,6},{8,9},{9,8},{10,11... | collective-permute-start | bytes 2359304 | tf_op jit(solution)/shard_map/ppermute | solution.py:586
  283.3 46.1 %all-to-all-start.2 = ((bf16[8,96,768]{2,1,0:T(8,128)(2,1)}), bf16[8,96,768]{2,1,0:T(8,128)(2,1)}, u32[]{:S(2)}, u32[]{:S(2)}) async-start(bf16[8,96,768]{2,1,0:T(8,128)(2,1)} %bitcast.92), calls=%async_computation.2 | async-start | bytes 2359296 | tf_op jit(solution)/shard_map/all_to_all | solution.py:604
  301.6 26.4 %collective-permute-start.50 = (bf16[768,768]{1,0:T(8,128)(2,1)S(1)}, bf16[768,768]{1,0:T(8,128)(2,1)S(1)}, u32[]{:S(2)}, u32[]{:S(2)}) collective-permute-start(bf16[768,768]{1,0:T(8,128)(2,1)S(1)} %slice_bitcast_fusion), channel_id=1, source_target_pairs={{0,2},{1,3},{2,0},{3,1},{4,6},{5,7},{6,4},{7,5},{8,10},{9,11},{10,... | collective-permute-start | bytes 3538952 | tf_op jit(solution)/shard_map/ppermute | solution.py:586
  304.9 32.7 %collective-permute-start.33 = (bf16[2,512,768]{2,1,0:T(8,128)(2,1)}, bf16[2,512,768]{2,1,0:T(8,128)(2,1)}, u32[]{:S(2)}, u32[]{:S(2)}) collective-permute-start(bf16[2,512,768]{2,1,0:T(8,128)(2,1)} %get-tuple-element.95), channel_id=1, source_target_pairs={{0,1},{1,0},{2,3},{3,2},{4,5},{5,4},{6,7},{7,6},{8,9},{9,8},{10,11... | collective-permute-start | bytes 4718600 | tf_op jit(solution)/shard_map/ppermute | solution.py:586
  304.9 32.7 %collective-permute-start.34 = (bf16[512,768]{1,0:T(8,128)(2,1)}, bf16[512,768]{1,0:T(8,128)(2,1)}, u32[]{:S(2)}, u32[]{:S(2)}) collective-permute-start(bf16[512,768]{1,0:T(8,128)(2,1)} %bitcast.2.tokens.right_a), channel_id=1, source_target_pairs={{0,1},{1,0},{2,3},{3,2},{4,5},{5,4},{6,7},{7,6},{8,9},{9,8},{10,11... | collective-permute-start | bytes 2359304 | tf_op jit(solution)/shard_map/ppermute | solution.py:586
  329.4 37.0 %all-to-all-start.3 = ((bf16[8,96,768]{2,1,0:T(8,128)(2,1)}), bf16[8,96,768]{2,1,0:T(8,128)(2,1)}, u32[]{:S(2)}, u32[]{:S(2)}) async-start(bf16[8,96,768]{2,1,0:T(8,128)(2,1)} %bitcast.93), calls=%async_computation.3 | async-start | bytes 2359296 | tf_op jit(solution)/shard_map/all_to_all | solution.py:604
  335.1 146.4 %all-gather.3.cloned.1.call-start = ((), (), s32[]{:S(2)}) async-start(), calls=%async_computation.4 | async-start | bytes 1327104 | tf_op jit(solution)/shard_map/all_gather | solution.py:606
  366.4 80.0 %all-to-all-start = ((bf16[8,72,768]{2,1,0:T(8,128)(2,1)}), bf16[8,72,768]{2,1,0:T(8,128)(2,1)}, u32[]{:S(2)}, u32[]{:S(2)}) async-start(bf16[8,72,768]{2,1,0:T(8,128)(2,1)} %bitcast.94), calls=%async_computation | async-start | bytes 1769472 | tf_op jit(solution)/shard_map/all_to_all | solution.py:604
  370.6 113.8 %all-gather.5.cloned.1.call-start = ((), (), s32[]{:S(2)}) async-start(), calls=%async_computation.5 | async-start | bytes 1327104 | tf_op jit(solution)/shard_map/all_gather | solution.py:606
  (98 other events, 1076.9 us)
Sparse Core Ops, SparseCore 0:
  338.2 60.4 all-gather.2
  400.8 40.6 all-gather.4

commit v2 on v1

v2 whole, which is shorter than its diff:
```python
import functools

import jax
import jax.numpy as jnp
from jax import lax
from jax.experimental import pallas as pl
from jax.experimental.pallas import tpu as pltpu
from jax.sharding import PartitionSpec as P

f32 = jnp.float32
bf16 = jnp.bfloat16
HEAD_DIM = 64
LANDMARKS = 64
NEWTON = 6
TAPS = 65
HALO = TAPS // 2
EARLY = 1
LATE = 0
GROUP = 256
NN = ((1,), (0,))
NT = ((1,), (1,))
TN = ((0,), (0,))
VMEM = pltpu.VMEM
ANY = pl.ANY


def dot(a, b, dims=NN):
    return lax.dot_general(a, b, (dims, ((), ())), preferred_element_type=f32)


def split(x):
    high = x.astype(bf16)
    return high, (x - high.astype(f32)).astype(bf16)


def mm(a, b, dims=NN):
    a_high, a_low = split(a)
    b_high, b_low = split(b)
    return dot(a_high, b_high, dims) + (dot(a_high, b_low, dims) + dot(a_low, b_high, dims))


def mm_left(a, b, dims=NN):
    a_high, a_low = split(a)
    return dot(a_high, b, dims) + dot(a_low, b, dims)


def iota(shape, dim):
    return lax.broadcasted_iota(jnp.int32, shape, dim)


def call(body, outs, ins, scratch=(), flops=0, size=0, limit=40, name=None, smem=()):
    specs = [
        pl.BlockSpec(memory_space=pltpu.SMEM) if i in smem else pl.BlockSpec(memory_space=space)
        for i, (space, _) in enumerate(ins)
    ]
    return pl.pallas_call(
        body,
        out_shape=[jax.ShapeDtypeStruct(s, d) for s, d in outs],
        in_specs=specs,
        out_specs=[pl.BlockSpec(memory_space=VMEM)] * len(outs),
        scratch_shapes=list(scratch),
        compiler_params=pltpu.CompilerParams(vmem_limit_bytes=limit << 20),
        cost_estimate=pl.CostEstimate(flops=flops, bytes_accessed=size, transcendentals=0),
        name=name,
    )(*[value for _, value in ins])


def call_many(parts, name):
    ins = [value for part in parts for value in part[2]]
    outs = [value for part in parts for value in part[1]]
    scratch = [value for part in parts for value in part[3]]
    smem, first = [], 0
    for part in parts:
        smem += [first + i for i in part[4]]
        first += len(part[2])

    def body(*refs):
        groups = [refs[: len(ins)], refs[len(ins) : len(ins) + len(outs)], refs[len(ins) + len(outs) :]]
        at = [0, 0, 0]
        for part in parts:
            mine = []
            for group, kind in ((0, 2), (1, 1), (2, 3)):
                mine += groups[group][at[group] : at[group] + len(part[kind])]
                at[group] += len(part[kind])
            part[0](*mine)

    results = call(body, outs, ins, scratch, flops=int(5e9), size=10 << 20, name=name, smem=tuple(smem), limit=48)
    split_results, first = [], 0
    for part in parts:
        split_results.append(results[first : first + len(part[1])])
        first += len(part[1])
    return split_results


def block_mask():
    return (iota((GROUP, GROUP), 0) >> 6) == (iota((GROUP, GROUP), 1) >> 6)


def spread(x):
    return jnp.where(block_mask(), jnp.concatenate([x, x, x, x], axis=0), 0.0)


def fold(x):
    kept = jnp.where(block_mask(), x, 0.0)
    return kept[0:64] + kept[64:128] + kept[128:192]


def rows_of(info, count, first):
    return info[1] + first + iota((count, 1), 0)


def landmark_kernel(p0, p1, wt, lm, chain):
    pooled = p0[...] + p1[...]
    high, low = split(pooled)
    both = jnp.concatenate([high, low], axis=0)
    lm[...] = jnp.zeros_like(lm)
    matrices, starts = [], []
    for head in range(3):
        pair = []
        for kind in range(2):
            rows = wt[kind * 192 + head * 64 : kind * 192 + head * 64 + 64]
            out = dot(both, rows, NT)
            out = out[0:64] + out[64:128]
            lm[:, kind * GROUP + head * 64 : kind * GROUP + head * 64 + 64] = out
            pair.append(out)
        scores = mm(pair[0], pair[1], NT) * 0.125
        raised = jnp.exp(scores - jnp.max(scores, axis=1, keepdims=True))
        matrix = raised / jnp.sum(raised, axis=1, keepdims=True)
        column = jnp.max(jnp.sum(matrix, axis=0, keepdims=True), axis=1, keepdims=True)
        row = jnp.max(jnp.sum(matrix, axis=1, keepdims=True), axis=0, keepdims=True)
        matrices.append(matrix)
        starts.append(matrix.T / (column * row))
    eye = (iota((64, 64), 0) == iota((64, 64), 1)).astype(f32)

    def step(it, iterates):
        results = []
        for head in range(3):
            z = iterates[head]
            product = mm(matrices[head], z)
            inner1 = 7.0 * eye - product
            inner2 = 15.0 * eye - mm(product, inner1)
            inner3 = 13.0 * eye - mm(product, inner2)
            chain[it, 0, head] = z
            chain[it, 1, head] = product
            chain[it, 2, head] = inner2
            chain[it, 3, head] = inner3
            results.append(0.25 * mm(z, inner3))
        return tuple(results)

    finals = lax.fori_loop(0, NEWTON, step, tuple(starts))
    for head in range(3):
        lm[:, 2 * GROUP + head * 64 : 2 * GROUP + head * 64 + 64] = finals[head]


def inverse_back_kernel(x0, x1, wst_all, lm, chain, partial, out):
    total = x0[0] + x1[1]
    eye = (iota((64, 64), 0) == iota((64, 64), 1)).astype(f32)
    weight = wst_all[0]
    out[...] = partial[...].astype(bf16)
    grads, matrices, queries, keys = [], [], [], []
    for head in range(3):
        at = slice(head * 64, head * 64 + 64)
        grads.append(mm(total[:, at], weight[:, at], NT))
        query = lm[:, head * 64 : head * 64 + 64]
        key = lm[:, GROUP + head * 64 : GROUP + head * 64 + 64]
        scores = mm(query, key, NT) * 0.125
        raised = jnp.exp(scores - jnp.max(scores, axis=1, keepdims=True))
        matrices.append(raised / jnp.sum(raised, axis=1, keepdims=True))
        queries.append(query)
        keys.append(key)

    def step(count, carried):
        it = NEWTON - 1 - count
        results = []
        for head in range(3):
            dz_next, da = carried[2 * head], carried[2 * head + 1]
            z = chain[it, 0, head]
            product = chain[it, 1, head]
            inner1 = 7.0 * eye - product
            inner2 = chain[it, 2, head]
            inner3 = chain[it, 3, head]
            dz_next = 0.25 * dz_next
            dz = mm(dz_next, inner3, NT)
            d3 = -mm(z, dz_next, TN)
            d2 = -mm(product, d3, TN)
            d1 = mm(product, d2, TN)
            dp = mm(d3, inner2, NT) + mm(d2, inner1, NT) - d1
            da = da + mm(dp, z, NT)
            dz = dz + mm(matrices[head], dp, TN)
            results += [dz, da]
        return tuple(results)

    first = []
    for head in range(3):
        first += [grads[head], jnp.zeros((64, 64), f32)]
    last = lax.fori_loop(0, NEWTON, step, tuple(first))
    for head in range(3):
        dz, da = last[2 * head], last[2 * head + 1]
        matrix = matrices[head]
        columns = jnp.sum(matrix, axis=0, keepdims=True)
        rows = jnp.sum(matrix, axis=1, keepdims=True)
        column = jnp.max(columns, axis=1, keepdims=True)
        row = jnp.max(rows, axis=0, keepdims=True)
        scale = 1.0 / (column * row)
        da = da + dz.T * scale
        d_scale = -jnp.sum(jnp.sum(dz * matrix.T, axis=1, keepdims=True), axis=0, keepdims=True) * scale * scale
        column_hit = (columns == column).astype(f32)
        row_hit = (rows == row).astype(f32)
        da = da + d_scale * row * column_hit / jnp.sum(column_hit, axis=1, keepdims=True)
        da = da + d_scale * column * row_hit / jnp.sum(row_hit, axis=0, keepdims=True)
        ds = matrix * (da - jnp.sum(da * matrix, axis=1, keepdims=True)) * 0.125
        for at, value in ((head * 64, mm(ds, keys[head])), (GROUP + head * 64, mm(ds, queries[head], TN))):
            out[0, :, at : at + 64] = (partial[0, :, at : at + 64] + value).astype(bf16)


PROJECTION = ((0, 192, 0), (192, 192, GROUP), (384, 192, 2 * GROUP))


def split_copies(refs, parts, held, sems, side):
    own, across, across_x, other, both, both_x = refs
    half = own.shape[1] // 2
    mine = pl.ds(pl.multiple_of(side * half, half), half)
    rest = pl.ds(pl.multiple_of((1 - side) * half, half), half)
    blocks = [[], [], [], []]
    for n, (row, rows, to) in enumerate(parts):
        first = pl.ds(row - parts[0][0], rows)
        source, to = pl.ds(row, rows), pl.ds(to, rows)
        blocks[0].append(pltpu.make_async_copy(own.at[first], held.at[0, to], sems.at[0, n, 0]))
        blocks[2].append(pltpu.make_async_copy(other.at[source], held.at[2, to], sems.at[2, n, 0]))
        for i, near, far in ((1, across, across_x), (3, both, both_x)):
            blocks[i].append(pltpu.make_async_copy(near.at[source], held.at[i, to, mine], sems.at[i, n, 0]))
            blocks[i].append(pltpu.make_async_copy(far.at[source], held.at[i, to, rest], sems.at[i, n, 1]))
    return blocks


def start(copies):
    for block in copies:
        for copy in block:
            copy.start()


def wait(copies, i):
    for block in range(4):

        @pl.when(i == block)
        def _():
            for copy in copies[block]:
                copy.wait()


def zero_gaps(held, kinds):
    for i in range(4):
        for kind in range(kinds):
            held[i, kind * GROUP + 192 : kind * GROUP + 256, :] = jnp.zeros((64, held.shape[2]), bf16)


def project_kernel(info, tokens, before, after, w0, w1, w2, w3, w4, w5, q_out, k_out, v_out, held, sems):
    count = tokens.shape[0]
    copies = split_copies((w0, w1, w2, w3, w4, w5), PROJECTION, held, sems, info[2])
    start(copies)
    zero_gaps(held, 3)
    valid = (rows_of(info, count, 0) < info[0]).astype(f32)
    valid_before = (rows_of(info, HALO, -HALO) < info[0]).astype(f32)
    valid_after = (rows_of(info, HALO, count) < info[0]).astype(f32)

    def body(i, _):
        wait(copies, i)
        for kind, out in ((0, q_out), (1, k_out)):
            out[i] = (dot(tokens[...], held[i, kind * GROUP : kind * GROUP + GROUP], NT) * valid).astype(bf16)
        wv = held[i, 2 * GROUP : 3 * GROUP]
        v_out[i, HALO : HALO + count] = (dot(tokens[...], wv, NT) * valid).astype(bf16)
        v_out[i, 0:HALO] = (dot(before[...], wv, NT) * valid_before).astype(bf16)
        v_out[i, HALO + count : 2 * HALO + count] = (dot(after[...], wv, NT) * valid_after).astype(bf16)
        v_out[i, 2 * HALO + count :] = jnp.zeros((v_out.shape[1] - 2 * HALO - count, GROUP), bf16)
        return 0

    lax.fori_loop(0, 4, body, 0)


def third_scores(info, lm, k_ref, i):
    count = k_ref.shape[1]
    valid = info[1] + iota((1, count), 1) < info[0]
    queries = spread(lm[i, :, 0:GROUP])
    return jnp.where(valid, mm_left(queries, k_ref[i], NT) * 0.125, -1e30)


def third_kernel(info, lm, k_ref, v_ref, pay):
    count = k_ref.shape[1]
    lane = iota((64, GROUP), 1)

    def body(i, _):
        scores = third_scores(info, lm, k_ref, i)
        top = jnp.max(scores, axis=1, keepdims=True)
        raised = jnp.exp(scores - top)
        total = jnp.sum(raised, axis=1, keepdims=True)
        packed = fold(mm_left(raised, v_ref[i, HALO : HALO + count]) / total)
        for stat, base in ((top, 192), (total, 216)):
            for term in range(3):
                part = stat.astype(bf16).astype(f32)
                stat = stat - part
                for head in range(3):
                    packed = jnp.where(lane == base + 8 * term + head, part[head * 64 : head * 64 + 64], packed)
        pay[i] = packed.astype(bf16)
        return 0

    lax.fori_loop(0, 4, body, 0)


def first_scores(lm, q_ref, i):
    keys = spread(lm[i, :, GROUP : 2 * GROUP])
    count = q_ref.shape[1]
    scores = (mm_left(keys, q_ref[i], NT) * 0.125).reshape(4, 64, count)
    raised = jnp.exp(scores - jnp.max(scores, axis=1, keepdims=True))
    return raised / jnp.sum(raised, axis=1, keepdims=True)


def toeplitz(row):
    return pltpu.roll(jnp.broadcast_to(row, (128, GROUP)), 0, 1, stride=1, stride_axis=0)


def head_select(x, rows):
    lane = iota((rows, GROUP), 1) >> 6
    out = jnp.where(lane == 0, x[0:rows], 0.0)
    out = jnp.where(lane == 1, x[rows : 2 * rows], out)
    return jnp.where(lane == 2, x[2 * rows : 3 * rows], out)


def context_kernel(p0, p1, p2, p3, lm, q_ref, v_ref, small, ctx, wst, x_out):
    count = q_ref.shape[1]
    lane = iota((64, GROUP), 1)

    def body(i, _):
        parts = [p[i ^ n].astype(f32) for n, p in enumerate((p0, p1, p2, p3))]

        def stat(part, at):
            return part[:, at : at + 1] + part[:, at + 8 : at + 9] + part[:, at + 16 : at + 17]

        factors = [jnp.zeros((64, GROUP), f32) for _ in range(4)]
        stats = jnp.zeros((64, GROUP), f32)
        for head in range(3):
            tops = [stat(part, 192 + head) for part in parts]
            top = jnp.maximum(jnp.maximum(tops[0], tops[1]), jnp.maximum(tops[2], tops[3]))
            scales = [stat(part, 216 + head) * jnp.exp(t - top) for part, t in zip(parts, tops)]
            total = sum(scales)
            mine = (lane >> 6) == head
            factors = [jnp.where(mine, s / total, f) for s, f in zip(scales, factors)]
            stats = jnp.where(lane == 192 + head, top, stats)
            stats = jnp.where(lane == 196 + head, total, stats)
        weight = sum(part * f for part, f in zip(parts, factors))
        wst[i] = jnp.where(lane < 192, weight, stats)
        mixed = mm(spread(lm[i, :, 2 * GROUP : 3 * GROUP]), spread(weight))
        x_out[i] = fold(mixed)
        first = first_scores(lm, q_ref, i).reshape(GROUP, count)
        main = mm(first, mixed, TN)
        bands = [toeplitz(small[i, 1 + head : 2 + head, 0:GROUP]) for head in range(3)]
        high, low = split(jnp.concatenate(bands, axis=0))
        for block in range(count // 128):
            window = v_ref[i, block * 128 : block * 128 + 256]
            conv = dot(high, window) + dot(low, window)
            ctx[i, block * 128 : block * 128 + 128] = (
                main[block * 128 : block * 128 + 128] + head_select(conv, 128)
            ).astype(bf16)
        return 0

    lax.fori_loop(0, 4, body, 0)


def first_back_kernel(
    info, g_ref, before, after, o0, o1, o2, o3, o4, o5, lm, q_ref, v_ref, small, x_in, dx, dq, dkl, dv, dtaps, held, sems, ext, dctx
):
    count = g_ref.shape[0]
    width = g_ref.shape[1]
    copies = split_copies((o0, o1, o2, o3, o4, o5), ((0, 192, 0),), held, sems, info[2])
    start(copies)
    zero_gaps(held, 1)
    valid = (rows_of(info, count, 0) < info[0]).astype(f32)
    ext[0:HALO] = before[...]
    ext[HALO : HALO + count] = g_ref[...]
    ext[HALO + count : 2 * HALO + count] = after[...]
    ext[2 * HALO + count :] = jnp.zeros((ext.shape[0] - 2 * HALO - count, width), bf16)
    lane = iota((128, GROUP), 1) >> 6
    flip = (iota((128, 128), 0) + iota((128, 128), 1) == 127).astype(bf16)

    def body(i, _):
        wait(copies, i)
        dctx[...] = dot(ext[...], held[i], NT)
        own = dctx[HALO : HALO + count]
        own_high = own.astype(bf16)
        first = first_scores(lm, q_ref, i)
        flat = first.reshape(GROUP, count)
        dx[i] = fold(dot(flat.astype(bf16), own_high))
        dfirst = dot(spread(x_in[i]).astype(bf16), own_high, NT)
        dfirst = dfirst.reshape(4, 64, count)
        ds = first * (dfirst - jnp.sum(first * dfirst, axis=1, keepdims=True)) * 0.125
        ds = ds.reshape(GROUP, count).astype(bf16)
        keys = (spread(lm[i, :, GROUP : 2 * GROUP])).astype(bf16)
        dquery = dot(ds, keys, TN)
        dq[i] = (dquery * valid).astype(bf16)
        dkl[i] = fold(dot(ds, q_ref[i]))
        bands = [toeplitz(small[i, 4 + head : 5 + head, 0:GROUP]) for head in range(3)]
        high = jnp.concatenate(bands, axis=0).astype(bf16)
        gram = jnp.zeros((384, GROUP), f32)
        for block in range(count // 128):
            conv = dot(high, dctx[block * 128 : block * 128 + 256].astype(bf16))
            dv[i, block * 128 : block * 128 + 128] = head_select(conv, 128)
            piece = dctx[HALO + block * 128 : HALO + block * 128 + 128]
            stacked = jnp.concatenate([jnp.where(lane == head, piece, 0.0) for head in range(3)], axis=0)
            gram = gram + dot(stacked.astype(bf16), v_ref[i, block * 128 : block * 128 + 256], NT)
        dtaps[i] = jnp.zeros((8, GROUP), f32)
        for head in range(3):
            part_high, part_low = split(gram[head * 128 : head * 128 + 128])
            upturned = dot(flip, part_high) + dot(flip, part_low)
            straight = pltpu.roll(upturned, GROUP - 127, 1, stride=1, stride_axis=0)
            summed = jnp.sum(straight, axis=0, keepdims=True)
            dtaps[i, 1 + head : 2 + head, :] = jnp.where(iota((1, GROUP), 1) < TAPS, summed, 0.0)
        return 0

    lax.fori_loop(0, 4, body, 0)


def third_back_kernel(info, x0, x1, lm, wst, k_ref, v_ref, dvc, dq, dkl, ctx, joint, send, partial):
    count = k_ref.shape[1]
    valid = (rows_of(info, count, 0) < info[0]).astype(f32)
    none = jnp.zeros((64, 1), f32)

    def body(i, _):
        dx = spread(x0[i] + x1[i ^ 1])
        dweight = mm(spread(lm[i, :, 2 * GROUP : 3 * GROUP]), dx, TN)
        stats = wst[i]
        weight = spread(jnp.where(iota((64, GROUP), 1) < 192, stats, 0.0))
        inner = jnp.sum(dweight * weight, axis=1, keepdims=True)
        top = jnp.concatenate([stats[:, 192 + head : 193 + head] for head in range(3)] + [none], axis=0)
        total = jnp.concatenate([stats[:, 196 + head : 197 + head] for head in range(3)] + [none + 1.0], axis=0)
        scores = third_scores(info, lm, k_ref, i)
        third = jnp.exp(scores - top) / total
        dw_high = dweight.astype(bf16)
        values = v_ref[i, HALO : HALO + count]
        dthird = dot(dw_high, values, NT)
        ds = (third * (dthird - inner) * 0.125).astype(bf16)
        queries = (spread(lm[i, :, 0:GROUP])).astype(bf16)
        dkey = dot(ds, queries, TN)
        partial[i, :, 0:GROUP] = fold(dot(ds, k_ref[i]))
        partial[i, :, GROUP : 2 * GROUP] = dkl[i]
        dvalues = dot(third.astype(bf16), dw_high, TN)
        joint[i, :, 0:GROUP] = dq[i]
        joint[i, :, GROUP : 2 * GROUP] = (dkey * valid).astype(bf16)
        joint[i, :, 2 * GROUP : 3 * GROUP] = ((dvalues + dvc[i]) * valid).astype(bf16)

        @pl.when(i >= 2)
        def _():
            send[i - 2, :, 0 : 3 * GROUP] = joint[i]
            send[i - 2, :, 3 * GROUP : 4 * GROUP] = ctx[i]

        return 0

    lax.fori_loop(0, 4, body, 0)


def token_back_kernel(info, l0, l1, joint, dres, w0, w1, w2, w3, w4, w5, out, held, sems):
    copies = split_copies((w0, w1, w2, w3, w4, w5), PROJECTION, held, sems, info[2])
    start(copies)
    zero_gaps(held, 3)
    count = joint.shape[1]
    mark = iota((1, 64), 1)
    low = (mark * info[0]) >> 6
    high = ((mark + 1) * info[0]) >> 6
    pos = rows_of(info, count, 0)
    member = ((pos >= low) & (pos < high)).astype(bf16)
    row = iota((64, 1), 0)
    width = ((((row + 1) * info[0]) >> 6) - ((row * info[0]) >> 6)).astype(f32)
    out[...] = dres[...]

    def body(i, pooled):
        wait(copies, i)
        out[...] += dot(joint[i], held[i])
        marks = (l0[i].astype(f32) + l1[i ^ 1].astype(f32)) / width
        return pooled + mm_left(marks, held[i, 0 : 2 * GROUP])

    pooled = lax.fori_loop(0, 4, body, jnp.zeros((64, out.shape[1]), f32))
    pooled_high, pooled_low = split(pooled)
    out[...] += dot(member, pooled_high) + dot(member, pooled_low)


def moments(x):
    centered = x - jnp.mean(x, axis=-1, keepdims=True)
    variance = jnp.mean(centered * centered, axis=-1, keepdims=True)
    inverse = lax.rsqrt(variance + 1e-05)
    return centered * inverse, inverse


def attended_kernel(info, ctx, tokens, gain, shift, o0, o1, o2, o3, o4, o5, pre, normed, low, held, sems):
    copies = split_copies((o0, o1, o2, o3, o4, o5), ((0, 192, 0),), held, sems, info[2])
    start(copies)
    zero_gaps(held, 1)
    pre[...] = tokens[...].astype(f32)

    def body(i, _):
        wait(copies, i)
        pre[...] += dot(ctx[i], held[i])
        return 0

    lax.fori_loop(0, 4, body, 0)
    unit, _ = moments(pre[...])
    result = unit * gain[...] + shift[...]
    normed[...] = result
    low[...] = result.astype(bf16)


def gelu_parts(u):
    cdf = 0.5 + 0.5 * lax.erf(u * 0.7071067811865476)
    pdf = jnp.exp(u * u * -0.5) * 0.3989422804014327
    return u * cdf, cdf + u * pdf


def up_kernel(info, low, small, w0, w1, w2, w3, w4, w5, hidden, slope, send, held, sems):
    copies = split_copies((w0, w1, w2, w3, w4, w5), ((192, held.shape[1], 0),), held, sems, info[2])
    start(copies)

    def body(i, _):
        wait(copies, i)
        for chunk in range(3):
            at = slice(chunk * 256, chunk * 256 + 256)
            upward = dot(low[...], held[i, :, at]) + small[i, 0:1, at]
            value, derivative = gelu_parts(upward)
            hidden[i, :, at] = value.astype(bf16)
            slope[i, :, at] = derivative.astype(bf16)

        @pl.when(i >= 2)
        def _():
            send[i - 2] = hidden[i]

        return 0

    send[2] = low[...]
    lax.fori_loop(0, 4, body, 0)


def norm_back(g, gain, unit, inverse):
    scaled = g * gain
    mean1 = jnp.mean(scaled, axis=-1, keepdims=True)
    mean2 = jnp.mean(scaled * unit, axis=-1, keepdims=True)
    return (scaled - mean1 - unit * mean2) * inverse


def down_kernel(info, hidden, normed, grad, gain, shift, w0, w1, w2, w3, w4, w5, out, dsum, dlow, sums, held, sems, acc):
    copies = split_copies((w0, w1, w2, w3, w4, w5), ((0, held.shape[1], 0),), held, sems, info[2])
    start(copies)
    acc[...] = normed[...]

    def body(i, _):
        wait(copies, i)
        acc[...] += dot(hidden[i], held[i])
        return 0

    lax.fori_loop(0, 4, body, 0)
    unit, inverse = moments(acc[...])
    out[...] = (unit * gain[...] + shift[...]).astype(bf16)
    g = grad[...].astype(f32)
    back = norm_back(g, gain[...], unit, inverse)
    dsum[...] = back
    dlow[...] = back.astype(bf16)
    sums[...] = jnp.zeros_like(sums)
    sums[0:1] = jnp.sum(g * unit, axis=0, keepdims=True)
    sums[1:2] = jnp.sum(g, axis=0, keepdims=True)


def hidden_back_kernel(info, dlow, slope, w0, w1, w2, w3, w4, w5, du, send, sums, held, sems):
    copies = split_copies((w0, w1, w2, w3, w4, w5), ((0, held.shape[1], 0),), held, sems, info[2])
    start(copies)
    sums[...] = jnp.zeros_like(sums)

    def body(i, _):
        wait(copies, i)
        for chunk in range(3):
            at = slice(chunk * 256, chunk * 256 + 256)
            back = dot(dlow[...], held[i, at, :], NT) * slope[i, :, at].astype(f32)
            back = back.astype(bf16)
            du[i, :, at] = back
            sums[i, 0:1, at] = jnp.sum(back.astype(f32), axis=0, keepdims=True)

        @pl.when(i >= 2)
        def _():
            send[i - 2] = du[i]

        return 0

    send[2] = dlow[...]
    lax.fori_loop(0, 4, body, 0)


def residual_back_kernel(info, du, dsum, pre, gain, w0, w1, w2, w3, w4, w5, dres, dlow, sums, held, sems, acc):
    copies = split_copies((w0, w1, w2, w3, w4, w5), ((192, held.shape[1], 0),), held, sems, info[2])
    start(copies)
    acc[...] = dsum[...]

    def body(i, _):
        wait(copies, i)
        acc[...] += dot(du[i], held[i], NT)
        return 0

    lax.fori_loop(0, 4, body, 0)
    unit, inverse = moments(pre[...])
    g = acc[...]
    back = norm_back(g, gain[...], unit, inverse)
    dres[...] = back
    dlow[...] = back.astype(bf16)
    sums[...] = jnp.zeros_like(sums)
    sums[0:1] = jnp.sum(g * unit, axis=0, keepdims=True)
    sums[1:2] = jnp.sum(g, axis=0, keepdims=True)


def feed_grad_kernel(
    pick, hidden, hidden_other, gd, du_other, du, low, down0, down1, up0, up1, left, right, sems
):
    half = left.shape[-1]
    copies = []

    def bring(source, target):
        copy = pltpu.make_async_copy(source, target, sems.at[len(copies)])
        copy.start()
        copies.append(copy)

    for part, sources in ((0, (hidden.at[0], hidden_other.at[0], hidden.at[1], hidden_other.at[1])), (1, (low, hidden_other.at[2]))):
        columns = pl.ds(pl.multiple_of(pick[part] * half, half), half)
        for n, source in enumerate(sources):
            bring(source.at[:, columns], left.at[4 * part + n])
        if part == 0:
            bring(gd, right.at[0])
            bring(du_other.at[2], right.at[1])
        else:
            for j in range(2):
                bring(du.at[j], right.at[2 + 2 * j])
                bring(du_other.at[j], right.at[3 + 2 * j])
    for copy in copies[:6]:
        copy.wait()
    for j, out in ((0, down0), (1, down1)):
        out[...] = (dot(left[2 * j], right[0], TN) + dot(left[2 * j + 1], right[1], TN)).astype(bf16)
    for copy in copies[6:]:
        copy.wait()
    for j, out in ((0, up0), (1, up1)):
        out[...] = (dot(left[4], right[2 + 2 * j], TN) + dot(left[5], right[3 + 2 * j], TN)).astype(bf16)


def feed_grad(pick, hidden, hidden_other, gd, du_other, du, low):
    count, width = gd.shape
    return (
        feed_grad_kernel,
        [((width // 2, width), bf16)] * 4,
        [(VMEM, pick.astype(jnp.int32))] + [(ANY, x) for x in (hidden, hidden_other, gd, du_other, du, low)],
        [
            pltpu.VMEM((6, count, width // 2), bf16),
            pltpu.VMEM((6, count, width), bf16),
            pltpu.SemaphoreType.DMA((12,)),
        ],
        (0,),
    )


def joint_grad_kernel(joint, other, ctx, tokens, tokens_other, g, g_other, first, second):
    for kind in range(4):
        at = slice(kind * GROUP, kind * GROUP + GROUP)
        if kind < 3:
            total = dot(joint[0, :, at], tokens[...], TN) + dot(other[0, :, at], tokens_other[...], TN)
        else:
            total = dot(ctx[0], g[...], TN) + dot(other[0, :, at], g_other[...], TN)
        out = first if kind < 2 else second
        out[kind % 2 * 192 : kind % 2 * 192 + 192] = total[0:192].astype(bf16)


def joint_grad(joint, other, ctx, tokens, tokens_other, g, g_other, block, name):
    count, width = tokens.shape
    whole = pl.BlockSpec((count, width), lambda j: (0, 0))
    return pl.pallas_call(
        joint_grad_kernel,
        grid=(1,),
        out_shape=[jax.ShapeDtypeStruct((width // 2, width), bf16)] * 2,
        in_specs=[
            pl.BlockSpec((1, count, 3 * GROUP), lambda j: (block, 0, 0)),
            pl.BlockSpec((1, count, 4 * GROUP), lambda j: (block, 0, 0)),
            pl.BlockSpec((1, count, GROUP), lambda j: (block, 0, 0)),
            whole,
            whole,
            whole,
            whole,
        ],
        out_specs=[pl.BlockSpec((width // 2, width), lambda j: (0, 0))] * 2,
        compiler_params=pltpu.CompilerParams(vmem_limit_bytes=40 << 20),
        cost_estimate=pl.CostEstimate(flops=16 * count * GROUP * width, bytes_accessed=8 << 20, transcendentals=0),
        name=name,
    )(joint, other, ctx, tokens, tokens_other, g, g_other)


HOP = {1: 2, 2: 1, 3: 3}


def hop(x, step):
    return lax.ppermute(x, "head", [(i, i ^ HOP[step]) for i in range(4)])


def after(x, *deps):
    return lax.optimization_barrier((x,) + deps)[0]


def local(
    batch_count,
    tokens,
    lengths,
    w_query,
    w_key,
    w_value,
    w_out,
    conv_taps,
    w_up,
    b_up,
    w_down,
    gain_attn,
    shift_attn,
    gain_ffn,
    shift_ffn,
    grad_out,
):
    tokens = tokens[0]
    grad_out = grad_out[0]
    count, width = tokens.shape
    ext = count + 128
    length = lengths[0]
    place = lax.axis_index("head")
    batch = lax.axis_index("batch")
    core = place & 1
    side = batch & 1
    info = jnp.stack([length, place * count, side]).astype(jnp.int32)
    gain_attn, shift_attn, gain_ffn, shift_ffn = (
        x.reshape(1, width) for x in (gain_attn, shift_attn, gain_ffn, shift_ffn)
    )
    vm, an = VMEM, ANY

    def hop_batch(x, step):
        return lax.ppermute(x, "batch", [(i, i ^ step) for i in range(batch_count)])

    def neighbours(x, other):
        first = core == 0
        far = lax.ppermute(jnp.where(first, x[:HALO], x[-HALO:]), "head", [(1, 2), (2, 1)])
        return jnp.where(first, far, other[-HALO:]), jnp.where(first, other[:HALO], far)

    marks = jnp.arange(LANDMARKS + 1, dtype=jnp.int32) * length // LANDMARKS
    positions = info[1] + jnp.arange(count, dtype=jnp.int32)
    member = (positions[None, :] >= marks[:-1, None]) & (positions[None, :] < marks[1:, None])
    pooled = jnp.dot(member.astype(bf16), tokens, preferred_element_type=f32)
    pooled = pooled / (marks[1:] - marks[:-1]).astype(f32)[:, None]
    pooled = pooled + hop(pooled, 2)
    pooled_across = hop(pooled, 1)

    taps = jnp.pad(conv_taps, ((0, 0), (0, width - TAPS)))
    taps_back = jnp.pad(conv_taps[:, ::-1], ((0, 0), (0, width - TAPS)))
    small_own = jnp.concatenate([b_up[None], taps, taps_back, jnp.zeros((1, width), f32)], axis=0)
    term1 = small_own.astype(bf16)
    rest = small_own - lax.reduce_precision(small_own, 8, 7)
    term2 = rest.astype(bf16)
    term3 = (rest - lax.reduce_precision(rest, 8, 7)).astype(bf16)
    wt_own = jnp.concatenate(
        [w_query.T, w_key.T, w_value.T, term1, term2, term3, jnp.zeros((8, width), bf16)], axis=0
    )
    tokens_other = hop(tokens, 2)
    before, behind = neighbours(tokens, tokens_other)

    def column_half(own):
        return lax.dynamic_slice_in_dim(own, side * (width // 2), width // 2, 1)

    wt_other = hop(wt_own, 2)
    wt_across = hop(column_half(wt_own), 1)
    lm_own, iterates = call(
        landmark_kernel,
        [((64, 3 * GROUP), f32), ((NEWTON, 4, 3, 64, 64), f32)],
        [(vm, pooled), (vm, pooled_across), (vm, wt_own)],
        flops=int(1e9),
        size=4 << 20,
        name="landmarks",
    )
    lm_across = hop(lm_own, 1)
    lm = jnp.stack([lm_own, lm_across, hop(lm_own, 2), hop(lm_across, 2)])
    pooled_low = (pooled + pooled_across).astype(bf16)
    wt_across_x = hop_batch(wt_across, 1)
    wt = [wt_own, wt_across, wt_across_x, wt_other, hop(wt_across, 2), hop(wt_across_x, 2)]

    def small_of(block):
        return sum(block[576 + 8 * n : 584 + 8 * n].astype(f32) for n in range(3))

    def small_joined(near, far):
        near, far = small_of(near), small_of(far)
        first = side == 0
        return jnp.concatenate([jnp.where(first, near, far), jnp.where(first, far, near)], axis=1)

    small = jnp.stack(
        [small_of(wt[0]), small_joined(wt[1], wt[2]), small_of(wt[3]), small_joined(wt[4], wt[5])]
    )
    out_up_own = jnp.concatenate([w_out, after(w_up, pooled)], axis=0)
    out_up_across = hop(after(column_half(out_up_own), pooled_across), 1)
    down_across = hop(after(column_half(w_down), lm_across), 1)
    q, k, v = call(
        project_kernel,
        [((4, count, GROUP), bf16), ((4, count, GROUP), bf16), ((4, ext, GROUP), bf16)],
        [(vm, info), (vm, tokens), (vm, before), (vm, behind)] + [(an, w) for w in wt],
        [pltpu.VMEM((4, 3 * GROUP, width), bf16), pltpu.SemaphoreType.DMA((4, 3, 2))],
        flops=2 * count * width * 3072,
        size=8 << 20,
        smem=(0,),
        name="project",
    )
    out_up_across_x = hop_batch(after(out_up_across, q), 1)
    (pay,) = call(
        third_kernel,
        [((4, 64, GROUP), bf16)],
        [(vm, info), (vm, lm), (vm, k), (vm, v)],
        flops=int(1e9),
        size=3 << 20,
        smem=(0,),
        name="third",
    )
    pays = [pay, hop(pay, 1), hop(pay, 2), hop(pay, 3)]
    ctx, wst, x_mid = call(
        context_kernel,
        [((4, count, GROUP), bf16), ((4, 64, GROUP), f32), ((4, 64, GROUP), f32)],
        [(vm, p) for p in pays] + [(vm, lm), (vm, q), (vm, v), (vm, small)],
        flops=int(3e9),
        size=5 << 20,
        name="context",
    )
    out_up_far = after((out_up_across, out_up_across_x), ctx)
    out_up = [out_up_across, out_up_across_x, hop(after(out_up_own, q), 2), hop(out_up_far[0], 2), hop(out_up_far[1], 2)]
    down_across_x = hop_batch(after(down_across, ctx), 1)
    wo = [(an, w) for w in [w_out] + out_up]
    wu = [(an, w) for w in [w_up] + out_up]
    out_scratch = [pltpu.VMEM((4, GROUP, width), bf16), pltpu.SemaphoreType.DMA((4, 1, 2))]
    wide = [pltpu.VMEM((4, width, width), bf16), pltpu.SemaphoreType.DMA((4, 1, 2))]
    acc = [pltpu.VMEM((count, width), f32)]

    pre, normed, normed_low = call(
        attended_kernel,
        [((count, width), f32), ((count, width), f32), ((count, width), bf16)],
        [(vm, info), (vm, ctx), (vm, tokens), (vm, gain_attn), (vm, shift_attn)] + wo,
        out_scratch,
        flops=2 * count * width * width,
        size=6 << 20,
        smem=(0,),
        name="attended",
    )
    down_far = after((down_across, down_across_x), normed_low)
    down = [down_across, down_across_x, hop(after(w_down, ctx), 2), hop(down_far[0], 2), hop(down_far[1], 2)]
    wd = [(an, w) for w in [w_down] + down]
    hidden, slope, hidden_send = call(
        up_kernel,
        [((4, count, width), bf16), ((4, count, width), bf16), ((3, count, width), bf16)],
        [(vm, info), (vm, normed_low), (vm, small)] + wu,
        wide,
        flops=2 * count * width * 3072,
        size=12 << 20,
        smem=(0,),
        name="up",
    )
    hidden_other = hop(hidden_send, 2)
    output, d_sum, gd, sums_ffn = call(
        down_kernel,
        [((count, width), bf16), ((count, width), f32), ((count, width), bf16), ((8, width), f32)],
        [(vm, info), (vm, hidden), (vm, normed), (vm, grad_out), (vm, gain_ffn), (vm, shift_ffn)] + wd,
        wide + acc,
        flops=2 * count * width * 3072,
        size=14 << 20,
        smem=(0,),
        name="down",
    )

    steps = [1 << n for n in range(batch_count.bit_length() - 1)]
    down_order = steps[:2] + ["y"] + steps[2:]
    up_order = steps[1:2] + steps[:1] + ["y"] + steps[2:]

    def bit(step):
        return (batch // step) & 1

    def send(x, step):
        return hop(x, 1) if step == "y" else hop_batch(x, step)

    def chain(pieces, step):
        received = [send(pieces[0], step)]
        for piece in pieces[1:]:
            received.append(send(after(piece, received[-1]), step))
        return received

    def add_all(kept, received):
        return [(a.astype(f32) + b.astype(f32)).astype(bf16) for a, b in zip(kept, received)]

    def split_for(pieces, step):
        if step == "y":
            return pieces[:1], pieces[1:]
        rows = pieces[0].shape[0] // 2
        kept = [lax.dynamic_slice_in_dim(x, bit(step) * rows, rows, 0) for x in pieces]
        sent = [lax.dynamic_slice_in_dim(x, (1 - bit(step)) * rows, rows, 0) for x in pieces]
        if len(pieces) > 1:
            sent = [jnp.stack(sent)]
        return kept, sent

    def exchange(pieces, step):
        kept, sent = split_for(pieces, step)
        received = send(sent[0], step)
        return kept, [received] if received.ndim == 2 else [received[n] for n in range(len(kept))]

    def grow(x, step):
        other = hop_batch(x, step)
        mine_last = bit(step) == 1
        return jnp.concatenate([jnp.where(mine_last, other, x), jnp.where(mine_last, x, other)], axis=0)

    def rest_of(order, done):
        back = [step for step in order if step != "y"][::-1]
        return [lambda x, step=step: add_all(*exchange(x, step)) for step in order[done:]] + [
            lambda x, step=step: [grow(x[0], step)] for step in back
        ]

    du, du_send, sums_up = call(
        hidden_back_kernel,
        [((4, count, width), bf16), ((3, count, width), bf16), ((4, 8, width), f32)],
        [(vm, info), (vm, gd), (vm, slope)] + wd,
        wide,
        flops=2 * count * width * 3072,
        size=12 << 20,
        smem=(0,),
        name="hidden_back",
    )
    du_other = hop(du_send, 2)
    mine = jnp.stack([bit(down_order[0]), bit(up_order[0])])
    operands = (hidden, hidden_other, gd, du_other, du, normed_low)
    ((down_sent0, down_sent1, up_sent0, up_sent1),) = call_many([feed_grad(1 - mine, *operands)], "grad_sent")
    down_first = send(down_sent0, down_order[0])
    up_first = send(up_sent0, up_order[0])
    kept, (d_res, ga, sums_attn) = call_many(
        [
            feed_grad(mine, hidden, hidden_other, after(gd, down_sent0), du_other, du, normed_low),
            (
                residual_back_kernel,
                [((count, width), f32), ((count, width), bf16), ((8, width), f32)],
                [(vm, info), (vm, du), (vm, d_sum), (vm, pre), (vm, gain_attn)] + wu,
                wide + acc,
                (0,),
            ),
        ],
        "grad_kept",
    )
    down_kept, up_kept = kept[:2], kept[2:]
    ga, down_first, up_first = after((ga, down_first, up_first), d_res)
    ga_other = hop(ga, 2)
    ga_before, ga_behind = neighbours(ga, ga_other)
    down_second = send(after(down_sent1, down_first), down_order[0])
    up_second = send(after(up_sent1, up_first), up_order[0])
    dx, dq, dkl, dv_conv, dtaps = call(
        first_back_kernel,
        [
            ((4, 64, GROUP), f32),
            ((4, count, GROUP), bf16),
            ((4, 64, GROUP), f32),
            ((4, count, GROUP), f32),
            ((4, 8, GROUP), f32),
        ],
        [(vm, info), (vm, after(ga, down_first, up_first)), (vm, ga_before), (vm, ga_behind)]
        + wo
        + [(vm, lm), (vm, q), (vm, v), (vm, small), (vm, x_mid)],
        out_scratch + [pltpu.VMEM((ext, width), bf16), pltpu.VMEM((ext, GROUP), f32)],
        flops=int(5e9),
        size=10 << 20,
        smem=(0,),
        name="first_back",
    )

    def swap_core(x):
        other = hop(x, 2)
        return x.astype(f32) + jnp.concatenate([other[2:4], other[0:2]], axis=0).astype(f32)

    dx, down_second, up_second = after((dx, down_second, up_second), dtaps)
    dx = swap_core(after(dx, down_second, up_second))
    down_sent, up_sent = [down_first, down_second], [up_first, up_second]
    d_down = exchange(add_all(down_kept, down_sent), down_order[1])
    d_up = exchange(add_all(up_kept, up_sent), up_order[1])
    dx_across = hop(dx, 1)
    dx, dx_across, d_down, d_up = after((dx, dx_across, d_down, d_up), dx_across)
    d_down = exchange(add_all(*d_down), down_order[2])
    d_up = exchange(add_all(*d_up), up_order[2])
    dx, dx_across = after((dx, dx_across), d_down[0], d_up[0])
    joint, joint_send, partial = call(
        third_back_kernel,
        [((4, count, 3 * GROUP), bf16), ((2, count, 4 * GROUP), bf16), ((4, 64, 2 * GROUP), f32)],
        [(vm, info), (vm, dx), (vm, dx_across), (vm, lm), (vm, wst), (vm, k), (vm, v), (vm, dv_conv), (vm, dq)]
        + [(vm, dkl), (vm, ctx)],
        flops=int(5e9),
        size=8 << 20,
        smem=(0,),
        name="third_back",
    )
    joint_other = hop(after(joint_send, d_down[1], d_up[1]), 2)
    d_down, d_up = after((d_down, d_up), partial)
    d_down, d_up = add_all(*d_down), add_all(*d_up)
    operands = (after(joint, *d_down, *d_up), joint_other, ctx, tokens, tokens_other, ga, ga_other)
    sent = joint_grad(*operands, 1, "grad_joint_sent")
    joint_first = send(sent[0], "y")
    d_down, d_up = after((d_down, d_up), *sent)
    d_down, d_up = exchange(d_down, down_order[3]), exchange(d_up, up_order[3])
    (partial,) = call(
        inverse_back_kernel,
        [((4, 64, 2 * GROUP), bf16)],
        [(vm, dx), (vm, dx_across), (vm, wst), (vm, lm_own), (vm, iterates), (vm, after(partial, *sent))],
        flops=int(1e9),
        size=4 << 20,
        name="inverse_back",
    )
    partial = after(partial, joint_first, d_down[1], d_up[1])
    d_down, d_up = after((d_down, d_up), partial)
    d_down, d_up = add_all(*d_down), add_all(*d_up)
    partial = swap_core(partial).astype(bf16)
    partial_across = hop(partial, 1)
    down_rest, up_rest = rest_of(down_order, 4), rest_of(up_order, 4)
    if EARLY >= 1:
        d_down, d_up = down_rest[0](d_down), up_rest[0](d_up)
        partial, partial_across = after((partial, partial_across), partial_across, d_down[0], d_up[0])
        down_rest, up_rest = down_rest[1:], up_rest[1:]
    else:
        partial, partial_across = after((partial, partial_across), partial_across)
    joint_second = send(after(sent[1], partial_across), "y")
    joint_sent = [joint_first, joint_second]
    joint_kept = joint_grad(*after(operands, partial), 0, "grad_joint_kept")
    if EARLY >= 2:
        d_down, d_up = down_rest[0](d_down), up_rest[0](d_up)
        down_rest, up_rest = down_rest[1:], up_rest[1:]
    (d_tokens,) = call(
        token_back_kernel,
        [((count, width), f32)],
        [(vm, info), (vm, partial), (vm, partial_across), (vm, joint), (vm, d_res)] + [(an, w) for w in wt],
        [pltpu.VMEM((4, 3 * GROUP, width), bf16), pltpu.SemaphoreType.DMA((4, 3, 2))],
        flops=2 * count * width * 3072,
        size=10 << 20,
        smem=(0,),
        name="token_back",
    )
    landmark_own = (partial[0].astype(f32) + partial_across[1].astype(f32)).astype(bf16)
    low_rank = dot(landmark_own, pooled_low, TN)
    low_rank = jnp.concatenate([low_rank[0:192], low_rank[GROUP : GROUP + 192]], axis=0)
    d_first = (joint_kept[0].astype(f32) + joint_sent[0].astype(f32) + low_rank).astype(bf16)
    d_second = (joint_kept[1].astype(f32) + joint_sent[1].astype(f32)).astype(bf16)
    norms = jnp.concatenate([sums_attn[0:2], sums_ffn[0:2]], axis=0)
    dtaps = jnp.pad(dtaps[:, 1:4], ((0, 0), (0, 0), (0, width - GROUP)))
    minor = jnp.concatenate([sums_up[:, 0:1], dtaps, jnp.broadcast_to(norms, (4, 4, width))], axis=1)
    minor = after(minor, joint_second)
    minor = minor[0:2] + hop(minor[2:4], 2)
    minor = minor[0] + hop(minor[1], 1)
    orders = [steps, steps[1:2] + steps[:1] + steps[2:]]
    values = [[d_first], [d_second], d_down, d_up, [minor]]
    tasks = [
        rest_of(orders[0], 0),
        rest_of(orders[1], 0),
        down_rest,
        up_rest,
        [lambda x: x] * LATE + [lambda x, step=step: [x[0] + hop_batch(x[0], step)] for step in steps],
    ]
    for turn in range(max(len(task) for task in tasks)):
        anchors = (values[0][0], values[1][0]) + ((d_tokens,) if turn == 0 else ())
        values = [
            task[turn](after(value, *anchors)) if turn < len(task) else value for value, task in zip(values, tasks)
        ]
    d_parts = [values[0][0].astype(f32), values[1][0].astype(f32)]
    d_w_down, d_w_up = values[2][0].astype(f32), values[3][0].astype(f32)
    minor = values[4][0]
    d_w_query, d_w_key = d_parts[0][0:192].T, d_parts[0][192:384].T
    d_w_value, d_w_out = d_parts[1][0:192].T, d_parts[1][192:384]

    return (
        output[None],
        d_tokens[None],
        d_w_query,
        d_w_key,
        d_w_value,
        d_w_out,
        minor[1:4, 0:TAPS],
        d_w_up,
        minor[0],
        d_w_down,
        minor[4],
        minor[5],
        minor[6],
        minor[7],
    )


def solution(mesh):
    return jax.shard_map(
        functools.partial(local, mesh.shape["batch"]),
        mesh=mesh,
        in_specs=(
            P("batch", "head", None),
            P("batch"),
            P(None, "head"),
            P(None, "head"),
            P(None, "head"),
            P("head", None),
            P("head", None),
            P(None, "head"),
            P("head"),
            P("head", None),
            P(),
            P(),
            P(),
            P(),
            P("batch", "head", None),
        ),
        out_specs=(
            P("batch", "head", None),
            P("batch", "head", None),
            P(None, "head"),
            P(None, "head"),
            P(None, "head"),
            P("head", None),
            P("head", None),
            P(None, "head"),
            P("head"),
            P("head", None),
            P(),
            P(),
            P(),
            P(),
        ),
        check_vma=False,
    )
```

time: 496 us -> 348 us (0.70)
  blocking collectives: 63.6 us -> 0 us
  starting transfers between devices: 102 us -> 61.8 us
  local copies, waits for them, and re-layouts: 40.2 us -> 26.5 us
  between operations: 15.7 us -> 3.36 us
  Pallas kernels: 111 us -> 104 us
  waiting for transfers between devices: 138 us -> 131 us
  other arithmetic: 21.9 us -> 14.9 us
    all_gather x2 -> x0, blocking collectives: 63.6 us -> none  [batch_total_large(): return lax.all_gather(piece, 'batch', axis=0, tiled=True)]
    ppermute x44 -> x35, waiting for transfers between devices: 116 us -> 53 us  [hop(): return lax.ppermute(x, 'head', [(i, i ^ HOP[step]) for i in range(4)])]
    ppermute x7 -> x34, waiting for transfers between devices: 17 us -> 78.4 us  [the longest x32 78.4 us: hop_batch(): return lax.ppermute(x, 'batch', [(i, i ^ step) for i in range(batch_count)])]
    ppermute x44 -> x35, starting transfers between devices: 67.1 us -> 23.4 us  [hop(): return lax.ppermute(x, 'head', [(i, i ^ HOP[step]) for i in range(4)])]
    ppermute x7 -> x34, starting transfers between devices: 14.5 us -> 38.4 us  [the longest x32 36.5 us: hop_batch(): return lax.ppermute(x, 'batch', [(i, i ^ step) for i in range(batch_count)])]
    all_to_all x4 -> x0, starting transfers between devices: 20 us -> none  [batch_total_large(): pieces = lax.all_to_all(x, 'batch', split_axis=0, concat_axis=0, tiled=True)]
    pallas_call x4 -> x2, Pallas kernels: 19.2 us -> 4.1 us  [joint_grad(): pl.pallas_call(joint_grad_kernel, grid=(1,), out_shape=[jax.ShapeDtypeStr...]
    unnamed x131 -> x190, local copies, waits for them, and re-layouts: 28 us -> 15.9 us
  transfers between devices with their start and end apart: 57 -> 69, of which waited for: 20 -> 34; matrix products, arithmetic and copies ran while one was open for 6% -> 7% of each run, Pallas kernels for 22% -> 28%
where the time goes in v2:
time: 348 us; the launch traced here: 345 us
  waiting for transfers between devices  131 us (38%)
  Pallas kernels  104 us (30%)
  starting transfers between devices  61.8 us (18%)
  local copies, waits for them, and re-layouts  26.5 us (8%)
  other arithmetic  14.9 us (4%)
    pallas_call x14, Pallas kernels, call(): pl.pallas_call(body, out_shape=[jax.ShapeDtypeStruct(s, d) for s, d in ou...  100 us
    ppermute x32, waiting for transfers between devices, hop_batch(): return lax.ppermute(x, 'batch', [(i, i ^ step) for i in range(batch_count)])  78.4 us
    ppermute x35, waiting for transfers between devices, hop(): return lax.ppermute(x, 'head', [(i, i ^ HOP[step]) for i in range(4)])  53 us
    ppermute x32, starting transfers between devices, hop_batch(): return lax.ppermute(x, 'batch', [(i, i ^ step) for i in range(batch_count)])  36.5 us
    ppermute x35, starting transfers between devices, hop(): return lax.ppermute(x, 'head', [(i, i ^ HOP[step]) for i in range(4)])  23.4 us
    unnamed x190, local copies, waits for them, and re-layouts  15.9 us
  transfers between devices with their start and end apart: 69, of which 34 were waited for; matrix products, arithmetic and copies ran while one was open for 7% of the time, Pallas kernels for 28%

profile of v2, /device:TPU:0, one launch (start us, length us, event | category | flops | bytes accessed | tf_op | source)
XLA Modules:
  0.0 344.7 jit_solution(17622451693012152175)
XLA Ops:
  12.7 11.7 %collective-permute-done.1.p1 = f32[64,768]{1,0:T(8,128)S(1)} collective-permute-done((f32[64,768]{1,0:T(8,128)S(1)}, f32[64,768]{1,0:T(8,128)S(1)}, u32[]{:S(2)}, u32[]{:S(2)}) %collective-permute-start.1) | collective-permute-done | bytes 196640 | tf_op jit(solution)/shard_map/ppermute | solution.py:697
  24.4 8.7 %landmarks.1 = (f32[64,768]{1,0:T(8,128)S(1)}, f32[6,4,3,64,64]{4,3,2,1,0:T(8,128)S(1)}) custom-call(f32[64,768]{1,0:T(8,128)S(1)} %add.219.p0, f32[64,768]{1,0:T(8,128)S(1)} %collective-permute-done.1.p1, bf16[608,768]{1,0:T(8,128)(2,1)S(1)} %constant_dynamic-update-slice_fusion.wt.w0), custom_call_target="tpu_custom_call" | custom-call | flops 1000000000 | bytes 4194304 | tf_op jit(solution)/shard_map/landmarks/pallas_call | solution.py:56
  35.0 4.7 %collective-permute-done.2 = f32[64,768]{1,0:T(8,128)S(1)} collective-permute-done((f32[64,768]{1,0:T(8,128)S(1)}, f32[64,768]{1,0:T(8,128)S(1)}, u32[]{:S(2)}, u32[]{:S(2)}) %collective-permute-start.2) | collective-permute-done | bytes 196640 | tf_op jit(solution)/shard_map/ppermute | solution.py:697
  47.4 5.8 %collective-permute-done.8.w2 = bf16[608,384]{1,0:T(8,128)(2,1)S(1)} collective-permute-done((bf16[608,384]{1,0:T(8,128)(2,1)}, bf16[608,384]{1,0:T(8,128)(2,1)S(1)}, u32[]{:S(2)}, u32[]{:S(2)}) %collective-permute-start.8) | collective-permute-done | bytes 466976 | tf_op jit(solution)/shard_map/ppermute | solution.py:738
  55.1 5.3 %project.1 = (bf16[4,512,256]{2,1,0:T(8,128)(2,1)S(1)}, bf16[4,512,256]{2,1,0:T(8,128)(2,1)S(1)}, bf16[4,640,256]{2,1,0:T(8,128)(2,1)S(1)}) custom-call(s32[3]{0:T(128)S(1)} %pad_add_fusion.info.refs_7_, bf16[512,768]{1,0:T(8,128)(2,1)S(1)} %bitcast.67, bf16[32,768]{1,0:T(8,128)(2,1)S(1)} %get-tuple-element.282.before, ...), custom_call_target="tpu_custom_call" | custom-call | flops 2415919104 | bytes 8388608 | tf_op jit(solution)/shard_map/project/pallas_call | solution.py:56
  76.2 6.7 %context.1 = (bf16[4,512,256]{2,1,0:T(8,128)(2,1)S(1)}, f32[4,64,256]{2,1,0:T(8,128)S(1)}, f32[4,64,256]{2,1,0:T(8,128)S(1)}) custom-call(bf16[4,64,256]{2,1,0:T(8,128)(2,1)S(1)} %third.1.p0, bf16[4,64,256]{2,1,0:T(8,128)(2,1)S(1)} %collective-permute-done.12.p1, bf16[4,64,256]{2,1,0:T(8,128)(2,1)S(1)} %collective-permute-done.13.p2, ...), custom_call_target="tpu_custom_call" | custom-call | flops 3000000000 | bytes 5242880 | tf_op jit(solution)/shard_map/context/pallas_call | solution.py:56
  84.9 4.3 %collective-permute-done.20.w1 = bf16[768,384]{1,0:T(8,128)(2,1)S(1)} collective-permute-done((bf16[768,384]{1,0:T(8,128)(2,1)S(1)}, bf16[768,384]{1,0:T(8,128)(2,1)S(1)}, u32[]{:S(2)}, u32[]{:S(2)}) %collective-permute-start.20) | collective-permute-done | bytes 589856 | tf_op jit(solution)/shard_map/ppermute | solution.py:697
  94.9 9.5 %collective-permute-done.21.w2 = bf16[768,384]{1,0:T(8,128)(2,1)S(1)} collective-permute-done((bf16[768,384]{1,0:T(8,128)(2,1)S(1)}, bf16[768,384]{1,0:T(8,128)(2,1)S(1)}, u32[]{:S(2)}, u32[]{:S(2)}) %collective-permute-start.21) | collective-permute-done | bytes 589856 | tf_op jit(solution)/shard_map/ppermute | solution.py:738
  105.0 8.7 %up.1 = (bf16[4,512,768]{2,1,0:T(8,128)(2,1)S(1)}, bf16[4,512,768]{2,1,0:T(8,128)(2,1)}, bf16[3,512,768]{2,1,0:T(8,128)(2,1)}) custom-call(s32[3]{0:T(128)S(1)} %pad_add_fusion.info.refs_7_, bf16[512,768]{1,0:T(8,128)(2,1)S(1)} %get-tuple-element.147.low.refs_6_, f32[4,8,768]{2,1,0:T(8,128)S(1)} %pad_maximum_fusion.11.small, ...), custom_call_target="tpu_custom_call" | custom-call | flops 2415919104 | bytes 12582912 | tf_op jit(solution)/shard_map/up/pallas_call | solution.py:56
  113.9 6.4 %down.1 = (bf16[512,768]{1,0:T(8,128)(2,1)}, f32[512,768]{1,0:T(8,128)S(1)}, bf16[512,768]{1,0:T(8,128)(2,1)S(1)}, f32[8,768]{1,0:T(8,128)S(1)}) custom-call(s32[3]{0:T(128)S(1)} %pad_add_fusion.info.refs_7_, bf16[4,512,768]{2,1,0:T(8,128)(2,1)S(1)} %get-tuple-element.148.hidden.refs_1_, f32[512,768]{1,0:T(8,128)S(1)} %get-tuple-element.149.normed, ...), custom_call_target="tpu_custom_call" | custom-call | flops 2415919104 | bytes 14680064 | tf_op jit(solution)/shard_map/down/pallas_call | solution.py:56
  121.5 6.4 %hidden_back.1 = (bf16[4,512,768]{2,1,0:T(8,128)(2,1)S(1)}, bf16[3,512,768]{2,1,0:T(8,128)(2,1)}, f32[4,8,768]{2,1,0:T(8,128)S(1)}) custom-call(s32[3]{0:T(128)S(1)} %pad_add_fusion.info.refs_7_, bf16[512,768]{1,0:T(8,128)(2,1)S(1)} %get-tuple-element.162.dlow.refs_3_, bf16[4,512,768]{2,1,0:T(8,128)(2,1)S(1)} %copy-done.71, bf16[768,768]{1,0:T(8,128)(2,1)S(1)} %copy-done.30, ...), custom_call_target="tpu_custom_call" | custom-call | flops 2415919104 | bytes 12582912 | tf_op jit(solution)/shard_map/hidden_back/pallas_call | solution.py:56
  138.1 5.8 %grad_sent.1 = (bf16[384,768]{1,0:T(8,128)(2,1)}, bf16[384,768]{1,0:T(8,128)(2,1)S(1)}, bf16[384,768]{1,0:T(8,128)(2,1)}, bf16[384,768]{1,0:T(8,128)(2,1)S(1)}) custom-call(s32[2]{0:T(128)S(1)} %get-tuple-element.263.refs_0_, bf16[4,512,768]{2,1,0:T(8,128)(2,1)} %copy-done.1, bf16[3,512,768]{2,1,0:T(8,128)(2,1)} %collective-permute-done.25.refs_2_, ...), custom_call_target="tpu_custom_call" | custom-call | flops 5000000000 | bytes 10485760 | tf_op jit(solution)/shard_map/grad_sent/pallas_call | solution.py:56
  148.7 13.6 %grad_kept.1 = (bf16[384,768]{1,0:T(8,128)(2,1)S(1)}, bf16[384,768]{1,0:T(8,128)(2,1)S(1)}, bf16[384,768]{1,0:T(8,128)(2,1)S(1)}, bf16[384,768]{1,0:T(8,128)(2,1...) custom-call(s32[2]{0:T(128)S(1)} %get-tuple-element.264.refs_0_, ...), custom_call_target="tpu_custom_call" | custom-call | flops 5000000000 | bytes 10485760 | tf_op jit(solution)/shard_map/grad_kept/pallas_call | solution.py:56
  169.0 9.6 %first_back.1 = (f32[4,64,256]{2,1,0:T(8,128)S(1)}, bf16[4,512,256]{2,1,0:T(8,128)(2,1)S(1)}, f32[4,64,256]{2,1,0:T(8,128)S(1)}, f32[4,512,256]{2,1,0:T(8,128)S(1)}, f32[4,8,256]{2,1,0:T(8,128)S(1)}) custom-call(s32[3]{0:T(128)S(1)} %pad_add_fusion.info.refs_7_, bf16[512,768]{1,0:T(8,128)(2,1)S(1)} %get-tuple-element.230.g_ref.g, ...), custom_call_target="tpu_custom_call" | custom-call | flops 5000000000 | bytes 10485760 | tf_op jit(solution)/shard_map/first_back/pallas_call | solution.py:56
  185.0 11.4 %collective-permute-done.35 = bf16[2,192,768]{2,1,0:T(8,128)(2,1)S(1)} collective-permute-done((bf16[2,192,768]{2,1,0:T(8,128)(2,1)S(1)}, bf16[2,192,768]{2,1,0:T(8,128)(2,1)S(1)}, u32[]{:S(2)}, u32[]{:S(2)}) %collective-permute-start.35) | collective-permute-done | bytes 589856 | tf_op jit(solution)/shard_map/ppermute | solution.py:738
  200.4 4.9 %third_back.1 = (bf16[4,512,768]{2,1,0:T(8,128)(2,1)S(1)}, bf16[2,512,1024]{2,1,0:T(8,128)(2,1)S(1)}, f32[4,64,512]{2,1,0:T(8,128)S(1)}) custom-call(s32[3]{0:T(128)S(1)} %pad_add_fusion.info.refs_7_, f32[4,64,256]{2,1,0:T(8,128)S(1)} %maximum_add_fusion.1.x0, f32[4,64,256]{2,1,0:T(8,128)S(1)} %collective-permute-done.34.x1, f32[4,64,768]{2,1,0:T(8,128)S(1)} %copy-done.44, ...), custom_call_target="tpu_custom_call" | custom-call | flops 5000000000 | bytes 8388608 | tf_op jit(solution)/shard_map/third_back/pallas_call | solution.py:56
  208.2 4.9 %collective-permute-done.37 = bf16[192,768]{1,0:T(8,128)(2,1)S(1)} collective-permute-done((bf16[192,768]{1,0:T(8,128)(2,1)S(1)}, bf16[192,768]{1,0:T(8,128)(2,1)S(1)}, u32[]{:S(2)}, u32[]{:S(2)}) %collective-permute-start.37) | collective-permute-done | bytes 294944 | tf_op jit(solution)/shard_map/ppermute | solution.py:697
  230.5 9.4 %inverse_back.1 = bf16[4,64,512]{2,1,0:T(8,128)(2,1)S(1)} custom-call(f32[4,64,256]{2,1,0:T(8,128)S(1)} %maximum_add_fusion.1.x0, f32[4,64,256]{2,1,0:T(8,128)S(1)} %copy-done.60, f32[4,64,256]{2,1,0:T(8,128)S(1)} %copy-done.58, f32[64,768]{1,0:T(8,128)S(1)} %copy-done.42, f32[6,4,3,64,64]{4,3,2,1,0:T(8,128)S(1)} %copy-done.32, f32[4,64,512]{2,1,0:T(8,128)S(1)} %copy-done.49), custom_call_target="tpu_custom_call" | custom-call | flops 1000000000 | bytes 4194304 | tf_op jit(solution)/shard_map/inverse_back/pallas_call | solution.py:56
  243.9 10.4 %collective-permute-done.46 = bf16[96,768]{1,0:T(8,128)(2,1)S(1)} collective-permute-done((bf16[96,768]{1,0:T(8,128)(2,1)S(1)}, bf16[96,768]{1,0:T(8,128)(2,1)S(1)}, u32[]{:S(2)}, u32[]{:S(2)}) %collective-permute-start.46) | collective-permute-done | bytes 147488 | tf_op jit(solution)/shard_map/ppermute | solution.py:738
  258.2 4.6 %collective-permute-done.44.l1 = bf16[4,64,512]{2,1,0:T(8,128)(2,1)S(1)} collective-permute-done((bf16[4,64,512]{2,1,0:T(8,128)(2,1)S(1)}, bf16[4,64,512]{2,1,0:T(8,128)(2,1)S(1)}, u32[]{:S(2)}, u32[]{:S(2)}) %collective-permute-start.44) | collective-permute-done | bytes 262176 | tf_op jit(solution)/shard_map/ppermute | solution.py:697
  263.1 7.6 %token_back.1 = f32[512,768]{1,0:T(8,128)} custom-call(s32[3]{0:T(128)S(1)} %pad_add_fusion.info.refs_7_, bf16[4,64,512]{2,1,0:T(8,128)(2,1)S(1)} %add_convert_fusion.13.l0, bf16[4,64,512]{2,1,0:T(8,128)(2,1)S(1)} %collective-permute-done.44.l1, bf16[4,512,768]{2,1,0:T(8,128)(2,1)S(1)} %get-tuple-element.225.joint, f32[512,768]{1,0:T(8,128)S(1)} %copy-done.35, ...), custom_call_target="tpu_custom_call" | custom-call | flops 2415919104 | bytes 10485760 | tf_op jit(solution)/shard_map/token_back/pallas_call | solution.py:56
  300.8 5.1 %collective-permute-done.53 = bf16[48,768]{1,0:T(8,128)(2,1)S(1)} collective-permute-done((bf16[48,768]{1,0:T(8,128)(2,1)S(1)}, bf16[48,768]{1,0:T(8,128)(2,1)S(1)}, u32[]{:S(2)}, u32[]{:S(2)}) %collective-permute-start.53) | collective-permute-done | bytes 73760 | tf_op jit(solution)/shard_map/ppermute | solution.py:738
  310.0 5.1 %collective-permute-done.54 = bf16[48,768]{1,0:T(8,128)(2,1)S(1)} collective-permute-done((bf16[48,768]{1,0:T(8,128)(2,1)S(1)}, bf16[48,768]{1,0:T(8,128)(2,1)S(1)}, u32[]{:S(2)}, u32[]{:S(2)}) %collective-permute-start.54) | collective-permute-done | bytes 73760 | tf_op jit(solution)/shard_map/ppermute | solution.py:738
  323.3 11.0 %collective-permute-done.57 = bf16[96,768]{1,0:T(8,128)(2,1)S(1)} collective-permute-done((bf16[96,768]{1,0:T(8,128)(2,1)S(1)}, bf16[96,768]{1,0:T(8,128)(2,1)S(1)}, u32[]{:S(2)}, u32[]{:S(2)}) %collective-permute-start.57) | collective-permute-done | bytes 147488 | tf_op jit(solution)/shard_map/ppermute | solution.py:738
  (440 shorter events, 159.8 us)
Async XLA Ops:
  4.2 43.3 %collective-permute-start.6 = (bf16[512,768]{1,0:T(8,128)(2,1)S(1)}, bf16[512,768]{1,0:T(8,128)(2,1)S(1)}, u32[]{:S(2)}, u32[]{:S(2)}) collective-permute-start(bf16[512,768]{1,0:T(8,128)(2,1)S(1)} %bitcast.66), channel_id=1, source_target_pairs={{0,1},{1,0},{2,3},{3,2},{4,5},{5,4},{6,7},{7,6},{8,9},{9,8},{10,11... | collective-permute-start | bytes 2359304 | tf_op jit(solution)/shard_map/ppermute | solution.py:697
  4.8 49.3 %collective-permute-start.9 = (bf16[608,768]{1,0:T(8,128)(2,1)S(1)}, bf16[608,768]{1,0:T(8,128)(2,1)}, u32[]{:S(2)}, u32[]{:S(2)}) collective-permute-start(bf16[608,768]{1,0:T(8,128)(2,1)S(1)} %constant_dynamic-update-slice_fusion.wt.w0), channel_id=1, source_target_pairs={{0,1},{1,0},{2,3},{3,2},{4,5},{5,4},{6,7},{7,6},{8,9},{9,8},{10,11... | collective-permute-start | bytes 2801672 | tf_op jit(solution)/shard_map/ppermute | solution.py:697
  6.1 33.8 %collective-permute-start.7 = (bf16[608,384]{1,0:T(8,128)(2,1)}, bf16[608,384]{1,0:T(8,128)(2,1)}, u32[]{:S(2)}, u32[]{:S(2)}) collective-permute-start(bf16[608,384]{1,0:T(8,128)(2,1)} %constant_dynamic-slice_fusion.16), channel_id=1, source_target_pairs={{0,2},{1,3},{2,0},{3,1},{4,6},{5,7},{6,4},{7,5},{8,10},{9,11},{10,... | collective-permute-start | bytes 1400840 | tf_op jit(solution)/shard_map/ppermute | solution.py:697
  42.7 19.7 %collective-permute-start.15 = (bf16[960,384]{1,0:T(8,128)(2,1)S(1)}, bf16[960,384]{1,0:T(8,128)(2,1)S(1)}, u32[]{:S(2)}, u32[]{:S(2)}) collective-permute-start(bf16[960,384]{1,0:T(8,128)(2,1)S(1)} %constant_dynamic-slice_fusion.15), channel_id=1, source_target_pairs={{0,2},{1,3},{2,0},{3,1},{4,6},{5,7},{6,4},{7,5},{8,10},{9,11},{10,... | collective-permute-start | bytes 2211848 | tf_op jit(solution)/shard_map/ppermute | solution.py:697
  62.4 22.0 %collective-permute-start.16 = (bf16[960,384]{1,0:T(8,128)(2,1)S(1)}, bf16[960,384]{1,0:T(8,128)(2,1)S(1)}, u32[]{:S(2)}, u32[]{:S(2)}) collective-permute-start(bf16[960,384]{1,0:T(8,128)(2,1)S(1)} %collective-permute-done.15.o1.w1.refs_13_), channel_id=1, source_target_pairs={{0,4},{4,0},{8,12},{12,8},{16,20},{20,16},{24,28},{28,24},{1,5},{5... | collective-permute-start | bytes 2211848 | tf_op jit(solution)/shard_map/ppermute | solution.py:738
  63.0 27.8 %collective-permute-start.17 = (bf16[960,768]{1,0:T(8,128)(2,1)S(1)}, bf16[960,768]{1,0:T(8,128)(2,1)S(1)}, u32[]{:S(2)}, u32[]{:S(2)}) collective-permute-start(bf16[960,768]{1,0:T(8,128)(2,1)S(1)} %constant_dynamic-update-slice_fusion.4), channel_id=1, source_target_pairs={{0,1},{1,0},{2,3},{3,2},{4,5},{5,4},{6,7},{7,6},{8,9},{9,8},{10,11... | collective-permute-start | bytes 4423688 | tf_op jit(solution)/shard_map/ppermute | solution.py:697
  73.1 16.1 %collective-permute-start.20 = (bf16[768,384]{1,0:T(8,128)(2,1)S(1)}, bf16[768,384]{1,0:T(8,128)(2,1)S(1)}, u32[]{:S(2)}, u32[]{:S(2)}) collective-permute-start(bf16[768,384]{1,0:T(8,128)(2,1)S(1)} %copy-done.83), channel_id=1, source_target_pairs={{0,2},{1,3},{2,0},{3,1},{4,6},{5,7},{6,4},{7,5},{8,10},{9,11},{10,... | collective-permute-start | bytes 1769480 | tf_op jit(solution)/shard_map/ppermute | solution.py:697
  89.2 15.2 %collective-permute-start.21 = (bf16[768,384]{1,0:T(8,128)(2,1)S(1)}, bf16[768,384]{1,0:T(8,128)(2,1)S(1)}, u32[]{:S(2)}, u32[]{:S(2)}) collective-permute-start(bf16[768,384]{1,0:T(8,128)(2,1)S(1)} %collective-permute-done.20.w1), channel_id=1, source_target_pairs={{0,4},{4,0},{8,12},{12,8},{16,20},{20,16},{24,28},{28,24},{1,5},{5... | collective-permute-start | bytes 1769480 | tf_op jit(solution)/shard_map/ppermute | solution.py:738
  90.7 23.1 %collective-permute-start.22 = (bf16[768,768]{1,0:T(8,128)(2,1)S(1)}, bf16[768,768]{1,0:T(8,128)(2,1)S(1)}, u32[]{:S(2)}, u32[]{:S(2)}) collective-permute-start(bf16[768,768]{1,0:T(8,128)(2,1)S(1)} %copy-done.30), channel_id=1, source_target_pairs={{0,1},{1,0},{2,3},{3,2},{4,5},{5,4},{6,7},{7,6},{8,9},{9,8},{10,11... | collective-permute-start | bytes 3538952 | tf_op jit(solution)/shard_map/ppermute | solution.py:697
  113.7 16.4 %collective-permute-start.25 = (bf16[3,512,768]{2,1,0:T(8,128)(2,1)}, bf16[3,512,768]{2,1,0:T(8,128)(2,1)}, u32[]{:S(2)}, u32[]{:S(2)}) collective-permute-start(bf16[3,512,768]{2,1,0:T(8,128)(2,1)} %get-tuple-element.156), channel_id=1, source_target_pairs={{0,1},{1,0},{2,3},{3,2},{4,5},{5,4},{6,7},{7,6},{8,9},{9,8},{10,11... | collective-permute-start | bytes 7077896 | tf_op jit(solution)/shard_map/ppermute | solution.py:697
  145.6 16.7 %collective-permute-start.28 = (bf16[384,768]{1,0:T(8,128)(2,1)}, bf16[384,768]{1,0:T(8,128)(2,1)}, u32[]{:S(2)}, u32[]{:S(2)}) collective-permute-start(bf16[384,768]{1,0:T(8,128)(2,1)} %get-tuple-element.166), channel_id=1, source_target_pairs={{0,8},{4,12},{8,0},{12,4},{16,24},{20,28},{24,16},{28,20},{1,9},{5... | collective-permute-start | bytes 1769480 | tf_op jit(solution)/shard_map/ppermute | solution.py:738
  147.2 15.6 %collective-permute-start.27 = (bf16[384,768]{1,0:T(8,128)(2,1)}, bf16[384,768]{1,0:T(8,128)(2,1)}, u32[]{:S(2)}, u32[]{:S(2)}) collective-permute-start(bf16[384,768]{1,0:T(8,128)(2,1)} %get-tuple-element.161), channel_id=1, source_target_pairs={{0,4},{4,0},{8,12},{12,8},{16,20},{20,16},{24,28},{28,24},{1,5},{5... | collective-permute-start | bytes 1769480 | tf_op jit(solution)/shard_map/ppermute | solution.py:738
  163.5 15.1 %collective-permute-start.32 = (bf16[384,768]{1,0:T(8,128)(2,1)S(1)}, bf16[384,768]{1,0:T(8,128)(2,1)S(1)}, u32[]{:S(2)}, u32[]{:S(2)}) collective-permute-start(bf16[384,768]{1,0:T(8,128)(2,1)S(1)} %copy-done.70), channel_id=1, source_target_pairs={{0,8},{4,12},{8,0},{12,4},{16,24},{20,28},{24,16},{28,20},{1,9},{5... | collective-permute-start | bytes 1769480 | tf_op jit(solution)/shard_map/ppermute | solution.py:738
  164.0 14.9 %collective-permute-start.31 = (bf16[384,768]{1,0:T(8,128)(2,1)S(1)}, bf16[384,768]{1,0:T(8,128)(2,1)S(1)}, u32[]{:S(2)}, u32[]{:S(2)}) collective-permute-start(bf16[384,768]{1,0:T(8,128)(2,1)S(1)} %copy-done.68), channel_id=1, source_target_pairs={{0,4},{4,0},{8,12},{12,8},{16,20},{20,16},{24,28},{28,24},{1,5},{5... | collective-permute-start | bytes 1769480 | tf_op jit(solution)/shard_map/ppermute | solution.py:738
  181.1 15.3 %collective-permute-start.35 = (bf16[2,192,768]{2,1,0:T(8,128)(2,1)S(1)}, bf16[2,192,768]{2,1,0:T(8,128)(2,1)S(1)}, u32[]{:S(2)}, u32[]{:S(2)}) collective-permute-start(bf16[2,192,768]{2,1,0:T(8,128)(2,1)S(1)} %pad_maximum_fusion.1), channel_id=1, source_target_pairs={{0,8},{4,12},{8,0},{12,4},{16,24},{20,28},{24,16},{28,20},{1,9},{5... | collective-permute-start | bytes 1769480 | tf_op jit(solution)/shard_map/ppermute | solution.py:738
  182.8 15.0 %collective-permute-start.36 = (bf16[2,192,768]{2,1,0:T(8,128)(2,1)S(1)}, bf16[2,192,768]{2,1,0:T(8,128)(2,1)S(1)}, u32[]{:S(2)}, u32[]{:S(2)}) collective-permute-start(bf16[2,192,768]{2,1,0:T(8,128)(2,1)S(1)} %pad_maximum_fusion.2), channel_id=1, source_target_pairs={{0,4},{4,0},{8,12},{12,8},{16,20},{20,16},{24,28},{28,24},{1,5},{5... | collective-permute-start | bytes 1769480 | tf_op jit(solution)/shard_map/ppermute | solution.py:738
  183.9 14.0 %collective-permute-start.34 = (f32[4,64,256]{2,1,0:T(8,128)S(1)}, f32[4,64,256]{2,1,0:T(8,128)S(1)}, u32[]{:S(2)}, u32[]{:S(2)}) collective-permute-start(f32[4,64,256]{2,1,0:T(8,128)S(1)} %maximum_add_fusion.1.x0), channel_id=1, source_target_pairs={{0,2},{1,3},{2,0},{3,1},{4,6},{5,7},{6,4},{7,5},{8,10},{9,11},{10,... | collective-permute-start | bytes 786440 | tf_op jit(solution)/shard_map/ppermute | solution.py:697
  220.3 20.3 %collective-permute-start.40 = (bf16[384,768]{1,0:T(8,128)(2,1)}, bf16[384,768]{1,0:T(8,128)(2,1)}, u32[]{:S(2)}, u32[]{:S(2)}) collective-permute-start(bf16[384,768]{1,0:T(8,128)(2,1)} %get-tuple-element.213), channel_id=1, source_target_pairs={{0,2},{1,3},{2,0},{3,1},{4,6},{5,7},{6,4},{7,5},{8,10},{9,11},{10,... | collective-permute-start | bytes 1769480 | tf_op jit(solution)/shard_map/ppermute | solution.py:697
  224.7 15.2 %collective-permute-start.41 = (bf16[96,768]{1,0:T(8,128)(2,1)S(1)}, bf16[96,768]{1,0:T(8,128)(2,1)S(1)}, u32[]{:S(2)}, u32[]{:S(2)}) collective-permute-start(bf16[96,768]{1,0:T(8,128)(2,1)S(1)} %get-tuple-element.314), channel_id=1, source_target_pairs={{0,16},{4,20},{8,24},{12,28},{16,0},{20,4},{24,8},{28,12},{1,17},{... | collective-permute-start | bytes 442376 | tf_op jit(solution)/shard_map/ppermute | solution.py:738
  242.8 14.6 %collective-permute-start.45 = (bf16[96,768]{1,0:T(8,128)(2,1)S(1)}, bf16[96,768]{1,0:T(8,128)(2,1)S(1)}, u32[]{:S(2)}, u32[]{:S(2)}) collective-permute-start(bf16[96,768]{1,0:T(8,128)(2,1)S(1)} %add_convert_fusion.17), channel_id=1, source_target_pairs={{0,16},{4,20},{8,24},{12,28},{16,0},{20,4},{24,8},{28,12},{1,17},{... | collective-permute-start | bytes 442376 | tf_op jit(solution)/shard_map/ppermute | solution.py:738
  262.8 14.4 %collective-permute-start.47 = (bf16[384,768]{1,0:T(8,128)(2,1)S(1)}, bf16[384,768]{1,0:T(8,128)(2,1)S(1)}, u32[]{:S(2)}, u32[]{:S(2)}) collective-permute-start(bf16[384,768]{1,0:T(8,128)(2,1)S(1)} %copy-done.66), channel_id=1, source_target_pairs={{0,2},{1,3},{2,0},{3,1},{4,6},{5,7},{6,4},{7,5},{8,10},{9,11},{10,... | collective-permute-start | bytes 1769480 | tf_op jit(solution)/shard_map/ppermute | solution.py:697
  289.5 17.4 %collective-permute-start.63 = (f32[8,768]{1,0:T(8,128)S(1)}, f32[8,768]{1,0:T(8,128)S(1)}, u32[]{:S(2)}, u32[]{:S(2)}) collective-permute-start(f32[8,768]{1,0:T(8,128)S(1)} %add.272), channel_id=1, source_target_pairs={{0,8},{4,12},{8,0},{12,4},{16,24},{20,28},{24,16},{28,20},{1,9},{5... | collective-permute-start | bytes 73736 | tf_op jit(solution)/shard_map/ppermute | solution.py:738
  316.5 20.1 %collective-permute-start.68 = (bf16[384,768]{1,0:T(8,128)(2,1)S(1)}, bf16[384,768]{1,0:T(8,128)(2,1)S(1)}, u32[]{:S(2)}, u32[]{:S(2)}) collective-permute-start(bf16[384,768]{1,0:T(8,128)(2,1)S(1)} %pad_maximum_fusion.4), channel_id=1, source_target_pairs={{0,4},{4,0},{8,12},{12,8},{16,20},{20,16},{24,28},{28,24},{1,5},{5... | collective-permute-start | bytes 1769480 | tf_op jit(solution)/shard_map/ppermute | solution.py:738
  317.1 19.7 %collective-permute-start.66 = (bf16[384,768]{1,0:T(8,128)(2,1)S(1)}, bf16[384,768]{1,0:T(8,128)(2,1)S(1)}, u32[]{:S(2)}, u32[]{:S(2)}) collective-permute-start(bf16[384,768]{1,0:T(8,128)(2,1)S(1)} %pad_maximum_fusion.3), channel_id=1, source_target_pairs={{0,8},{4,12},{8,0},{12,4},{16,24},{20,28},{24,16},{28,20},{1,9},{5... | collective-permute-start | bytes 1769480 | tf_op jit(solution)/shard_map/ppermute | solution.py:738
  (138 other events, 1352.3 us)
